TPU v7x, 256 devices: a whole 4x4x8 slice. The times are simulated.
256 devices in a mesh: row: 8 (over z), col: 32 (over x, y, core).
Axes of the slice: x: 4, y: 4, z: 8, core: 2. Of those that a mesh axis runs over, the one named last changes fastest.
Arguments:
- forcing: float32 [3, 4096, 128], P(None, ('row', 'col')), may hold values from -27 to 27
- stiffness: float32 [4096], P(('row', 'col')), may hold values from 0.02 to 0.3
- positions: float32 [3, 4096], P(None, ('row', 'col')), may hold values from 0 to 1
- far_weights: float32 [128], replicated, may hold values from 0 to 0.015625
- far_profile: float32 [128], replicated, may hold values from 0.5 to 1.5
- near_blocks: bfloat16 [8192, 384, 384], P(('row', 'col')), may hold values from -0.125 to 0.125
- near_dest: int32 [8192, 1], P(('row', 'col')), may hold values from 0 to 31; in each aligned block of 32 rows (0 to 31, 32 to 63, ...) at most 2 rows name the same one
- near_cilia: int32 [8192, 2], P(('row', 'col')), may hold values from 0 to 15
- near_count: int32 [256], P(('row', 'col')), may hold values from 16 to 32, as said below
Outputs:
- solution: float32 [3, 4096, 128], P(None, ('row', 'col'))
- residual: float32 [3, 4096, 128], P(None, ('row', 'col'))
Inputs may be any that keep to these rules, and one draw needn't show every extreme that they name: `near_dest`: among the 32 slots of one device no index of col is named more than 2 times, and in every draw some device names one exactly 2 times. `near_cilia`: column 0 is the source cilium's place among its device's 16 cilia, column 1 the target cilium's place on its device. `near_count`: some device has all 32 slots live.
All inputs are finite; a program needn't handle non-finite values.
Results may differ from a plain program's by a relative error of at most 0.01.
Values may be sent and summed in bfloat16 or wider, within the bound.
No kernel may reach another device: no remote copies, remote signals or barrier semaphores. Data moves between devices by JAX's collectives and lax.ppermute only.
A program may use at most 192 MiB of HBM per device.

v0:
```python
import jax
import jax.numpy as jnp
from jax import lax
from jax.sharding import PartitionSpec as P

CAPD = 2
ITERS = 4


EPSILON = 1e-06


def bending(vector, stiffness):
    padded = jnp.pad(vector, ((0, 0), (0, 0), (2, 2)))
    fourth = (
        padded[:, :, :-4]
        - 4.0 * padded[:, :, 1:-3]
        + 6.0 * vector
        - 4.0 * padded[:, :, 3:-1]
        + padded[:, :, 4:]
    )
    return vector + stiffness[None, :, None] * fourth


def far_block(target_pos, source_pos, strengths, eps_two, eps_three):
    displacement = target_pos[:, :, None] - source_pos[:, None, :]
    inverse = 1.0 / (jnp.sum(displacement * displacement, axis=0) + eps_two)
    amplitude = eps_three * inverse * jnp.sqrt(inverse)
    projected = jnp.sum(displacement * strengths[:, None, :], axis=0) * inverse
    return jnp.sum(
        amplitude[None] * (strengths[:, None, :] + displacement * projected[None]), axis=2
    )


def far_tiles(target_pos, source_pos, strengths, eps_two, eps_three):
    target_total = target_pos.shape[1]
    tile_width = min(target_total, 128)
    target_tiles = target_pos.reshape(3, target_total // tile_width, tile_width).transpose(1, 0, 2)

    def one_tile(tile_pos):
        return far_block(tile_pos, source_pos, strengths, eps_two, eps_three)

    speeds = lax.map(one_tile, target_tiles)
    return speeds.transpose(1, 0, 2).reshape(3, target_total)


def back_substitute(triangle, target):
    answers = [None] * ITERS
    for index in reversed(range(ITERS)):
        running = target[index]
        for later in range(index + 1, ITERS):
            running = running - triangle[index, later] * answers[later]
        answers[index] = running / triangle[index, index]
    return jnp.stack(answers)


def least_squares(hessenberg, initial_norm):
    unit_columns = []
    triangle = jnp.zeros((ITERS, ITERS), jnp.float32)
    for column in range(ITERS):
        vector = hessenberg[:, column]
        for earlier in range(column):
            weight = jnp.sum(unit_columns[earlier] * vector)
            triangle = triangle.at[earlier, column].set(weight)
            vector = vector - weight * unit_columns[earlier]
        length = jnp.sqrt(jnp.sum(vector * vector))
        triangle = triangle.at[column, column].set(length)
        unit_columns.append(vector / length)
    target = initial_norm * jnp.stack([unit[0] for unit in unit_columns])
    return back_substitute(triangle, target)


def on_device(
    forcing,
    stiffness,
    positions,
    far_weights,
    far_profile,
    near_blocks,
    near_dest,
    near_cilia,
    near_count,
):
    row_count = lax.axis_size("row")
    col_count = lax.axis_size("col")
    cilia_dev = forcing.shape[1]
    points = forcing.shape[2]
    slot_total = near_blocks.shape[0]
    row_width = 3 * points
    eps_three = 4.0 / (cilia_dev * row_count * col_count)
    eps_two = eps_three ** (2.0 / 3.0)
    destination = near_dest[:, 0]
    active = lax.iota(jnp.int32, slot_total) < near_count[0]
    matches = (destination[:, None] == lax.iota(jnp.int32, col_count)[None, :]).astype(jnp.int32)
    ranking = jnp.sum((jnp.cumsum(matches, axis=0) - matches) * matches, axis=1)
    position = destination * CAPD + ranking
    buffer_len = col_count * CAPD
    placing = (position[None, :] == lax.iota(jnp.int32, buffer_len)[:, None]).astype(jnp.int32)
    anchor = jnp.sum(placing * lax.iota(jnp.int32, slot_total)[None, :], axis=1)
    filled = jnp.sum(placing * active.astype(jnp.int32)[None, :], axis=1) > 0
    target_sent = jnp.where(filled, jnp.take(near_cilia[:, 1], anchor), 0)
    source_local = near_cilia[:, 0]
    cilia_iota = lax.iota(jnp.int32, cilia_dev)
    flat_blocks = near_blocks.reshape(slot_total, row_width * row_width)
    block_rows = jnp.where(
        filled[:, None], jnp.take(flat_blocks, anchor, axis=0), jnp.zeros((), jnp.bfloat16)
    )
    received_blocks, received_targets = (
        lax.all_to_all(block_rows, "col", split_axis=0, concat_axis=0, tiled=True),
        lax.all_to_all(target_sent, "col", split_axis=0, concat_axis=0, tiled=True),
    )
    received_blocks = received_blocks.reshape(buffer_len, row_width, row_width)
    gathering = (received_targets[None, :] == cilia_iota[:, None]).astype(jnp.float32)

    def near_field(vector):
        row_table = vector.transpose(1, 0, 2).reshape(cilia_dev, row_width)
        sources = jnp.take(row_table, source_local, axis=0).astype(jnp.bfloat16)
        outgoing = jnp.take(sources, anchor, axis=0)
        incoming = lax.all_to_all(outgoing, "col", split_axis=0, concat_axis=0, tiled=True)
        speeds = jnp.einsum(
            "kij,kj->ki", received_blocks, incoming, preferred_element_type=jnp.float32
        )
        summed = jnp.dot(gathering, speeds, precision=lax.Precision.HIGHEST)
        return summed.reshape(cilia_dev, 3, points).transpose(1, 0, 2)

    target_pos = lax.all_gather(positions, "row", axis=1, tiled=True)
    source_pos = lax.all_gather(positions, "col", axis=1, tiled=True)

    def far_field(vector):
        strengths = jnp.sum(vector * far_weights[None, None, :], axis=2)
        partial_speeds = far_tiles(
            target_pos,
            source_pos,
            lax.all_gather(strengths, "col", axis=1, tiled=True),
            eps_two,
            eps_three,
        )
        speeds = lax.psum_scatter(partial_speeds, "row", scatter_dimension=1, tiled=True)
        return speeds[:, :, None] * far_profile[None, None, :]

    def operator(vector):
        return bending(vector, stiffness) + near_field(vector) + far_field(vector)

    def norm_of(vector):
        return jnp.sqrt(lax.psum(jnp.sum(vector * vector), ("row", "col")) + EPSILON)

    initial_norm = norm_of(forcing)
    basis = [forcing / initial_norm]
    hessenberg = jnp.zeros((ITERS + 1, ITERS), jnp.float32)
    for column in range(ITERS):
        image = operator(basis[column])
        for earlier in range(column + 1):
            height = lax.psum(jnp.sum(basis[earlier] * image), ("row", "col"))
            image = image - height * basis[earlier]
            hessenberg = hessenberg.at[earlier, column].set(height)
        length = norm_of(image)
        hessenberg = hessenberg.at[column + 1, column].set(length)
        basis.append(image / length)
    coefficients = least_squares(hessenberg, initial_norm)
    solution = coefficients[0] * basis[0]
    for column in range(1, ITERS):
        solution = solution + coefficients[column] * basis[column]
    residual = forcing - operator(solution)
    return (solution, residual)


def solution(mesh):
    in_specs = (
        P(None, ("row", "col"), None),
        P(("row", "col")),
        P(None, ("row", "col")),
        P(),
        P(),
        P(("row", "col"), None, None),
        P(("row", "col"), None),
        P(("row", "col"), None),
        P(("row", "col")),
    )
    out_specs = (P(None, ("row", "col"), None), P(None, ("row", "col"), None))
    return jax.shard_map(
        on_device, mesh=mesh, in_specs=in_specs, out_specs=out_specs, check_vma=False
    )
```

profile of v0, /device:TPU:1, one launch (start us, length us, event | category | flops | bytes accessed | tf_op | source)
XLA Modules:
  0.0 2044.6 jit_solution(6894117404861532692)
XLA Ops:
  12.7 8.6 all-to-all-start
  23.4 80.4 %psum.105 = f32[]{:T(128)} all-reduce(f32[]{:T(128)} %multiply_reduce_fusion.19), channel_id=1, replica_groups=mesh['row'=8,'col'=32] {'row','col'}, use_global_device_ids=true, to_apply=%region_1.2 | all-reduce | flops 1 | bytes 8 | tf_op jit(solution)/shard_map/psum | solution.py:145
  104.5 13.0 copy.114
  117.5 8.0 fusion.106
  125.5 21.2 %gather_fusion.2 = bf16[64,73728]{1,0:T(8,128)(2,1)} fusion(bf16[32,73728]{1,0:T(8,128)(2,1)} %get-tuple-element.423, s32[1024]{0:T(1024)S(1)} %pad_clamp_fusion.2), kind=kCustom, calls=%fused_computation.12 | custom fusion | bytes 18874624 | tf_op jit(solution)/shard_map/jit(_take)/gather | solution.py:106
  146.8 21.6 %gather_fusion.1 = bf16[64,73728]{1,0:T(8,128)(2,1)} fusion(bf16[32,73728]{1,0:T(8,128)(2,1)} %get-tuple-element.422, s32[1024]{0:T(1024)S(1)} %pad_clamp_fusion.2), kind=kCustom, calls=%fused_computation.11 | custom fusion | bytes 18874624 | tf_op jit(solution)/shard_map/jit(_take)/gather | solution.py:106
  168.6 19.4 pad_maximum_fusion
  189.6 18.6 gather.21
  208.8 4.4 all-to-all-start.2
  213.3 23.9 %broadcast_select_fusion.1 = bf16[32,2,147456]{2,1,0:T(2,128)(2,1)} fusion(pred[32,2]{1,0:T(8,128)(4,1)S(1)} %gt.34, bf16[32,2,147456]{2,1,0:T(2,128)(2,1)} %gather.21, pred[32,2]{1,0:T(8,128)(4,1)S(1)} %compare_and_fusion), kind=kLoop, calls=%fused_computation.14 | loop fusion | flops 18874368 | bytes 37748864 | tf_op jit(solution)/shard_map/jit(_where)/select_n | solution.py:105
  237.2 7.6 all-to-all-start.1
  244.8 318.2 %all-gather.1 = f32[32,16,3]{1,2,0:T(4,128)S(1)} all-gather(f32[1,16,3]{1,2,0:T(4,128)S(1)} %bitcast.273), channel_id=1, replica_groups=mesh['row'=8,'col'=32] {'col'}, dimensions={0}, use_global_device_ids=true | all-gather | bytes 6336 | tf_op jit(solution)/shard_map/all_gather | solution.py:127
  563.1 15.5 all-gather
  578.7 30.4 %all-gather.2 = f32[32,16,3]{1,2,0:T(4,128)S(1)} all-gather(f32[1,16,3]{1,2,0:T(4,128)S(1)} %bitcast.275), channel_id=1, replica_groups=mesh['row'=8,'col'=32] {'col'}, dimensions={0}, use_global_device_ids=true | all-gather | bytes 6336 | tf_op jit(solution)/shard_map/all_gather | solution.py:134
  615.9 29.5 %reshape.929 = bf16[64,384,384]{2,1,0:T(8,128)(2,1)} reshape(bf16[32,2,147456]{2,1,0:T(2,128)(2,1)} %all-to-all-done.1) | data formatting | bytes 37748736 | tf_op jit(solution)/shard_map/reshape | solution.py:112
  645.4 9.3 fusion.112
  656.4 73.6 %psum.106 = f32[]{:T(128)} all-reduce(f32[]{:T(128)} %get-tuple-element.416), channel_id=1, replica_groups=mesh['row'=8,'col'=32] {'row','col'}, use_global_device_ids=true, to_apply=%region_12.15 | all-reduce | flops 1 | bytes 8 | tf_op jit(solution)/shard_map/psum | solution.py:153
  731.9 73.5 %psum.107 = f32[]{:T(128)} all-reduce(f32[]{:T(128)} %multiply_reduce_fusion.16), channel_id=1, replica_groups=mesh['row'=8,'col'=32] {'row','col'}, use_global_device_ids=true, to_apply=%region_14.17 | all-reduce | flops 1 | bytes 8 | tf_op jit(solution)/shard_map/psum | solution.py:145
  807.0 23.3 %all-gather.3 = f32[32,16,3]{1,2,0:T(4,128)S(1)} all-gather(f32[1,16,3]{1,2,0:T(4,128)S(1)} %bitcast.276), channel_id=1, replica_groups=mesh['row'=8,'col'=32] {'col'}, dimensions={0}, use_global_device_ids=true | all-gather | bytes 6336 | tf_op jit(solution)/shard_map/all_gather | solution.py:134
  832.7 4.3 all-to-all-start.3
  838.8 5.5 all-to-all-done.3
  844.4 9.3 fusion.113
  853.8 16.3 reduce-scatter.18.cloned.1.call-done
  871.6 80.2 %psum.108 = f32[]{:T(128)} all-reduce(f32[]{:T(128)} %get-tuple-element.412), channel_id=1, replica_groups=mesh['row'=8,'col'=32] {'row','col'}, use_global_device_ids=true, to_apply=%region_20.23 | all-reduce | flops 1 | bytes 8 | tf_op jit(solution)/shard_map/psum | solution.py:153
  953.2 73.4 %psum.109 = f32[]{:T(128)} all-reduce(f32[]{:T(128)} %multiply_reduce_fusion.13), channel_id=1, replica_groups=mesh['row'=8,'col'=32] {'row','col'}, use_global_device_ids=true, to_apply=%region_22.25 | all-reduce | flops 1 | bytes 8 | tf_op jit(solution)/shard_map/psum | solution.py:153
  1028.6 74.3 %psum.110 = f32[]{:T(128)} all-reduce(f32[]{:T(128)} %get-tuple-element.410), channel_id=1, replica_groups=mesh['row'=8,'col'=32] {'row','col'}, use_global_device_ids=true, to_apply=%region_24.27 | all-reduce | flops 1 | bytes 8 | tf_op jit(solution)/shard_map/psum | solution.py:145
  1103.7 23.7 %all-gather.4 = f32[32,16,3]{1,2,0:T(4,128)S(1)} all-gather(f32[1,16,3]{1,2,0:T(4,128)S(1)} %bitcast.277), channel_id=1, replica_groups=mesh['row'=8,'col'=32] {'col'}, dimensions={0}, use_global_device_ids=true | all-gather | bytes 6336 | tf_op jit(solution)/shard_map/all_gather | solution.py:134
  1129.9 4.3 all-to-all-start.4
  1138.0 3.5 all-to-all-done.4
  1141.6 9.3 fusion.114
  1151.0 16.4 reduce-scatter.20.cloned.1.call-done
  1168.9 80.3 %psum.111 = f32[]{:T(128)} all-reduce(f32[]{:T(128)} %get-tuple-element.406), channel_id=1, replica_groups=mesh['row'=8,'col'=32] {'row','col'}, use_global_device_ids=true, to_apply=%region_31.34 | all-reduce | flops 1 | bytes 8 | tf_op jit(solution)/shard_map/psum | solution.py:153
  1250.6 73.4 %psum.112 = f32[]{:T(128)} all-reduce(f32[]{:T(128)} %multiply_reduce_fusion.9), channel_id=1, replica_groups=mesh['row'=8,'col'=32] {'row','col'}, use_global_device_ids=true, to_apply=%region_33.36 | all-reduce | flops 1 | bytes 8 | tf_op jit(solution)/shard_map/psum | solution.py:153
  1327.9 74.3 %psum.113 = f32[]{:T(128)} all-reduce(f32[]{:T(128)} %multiply_reduce_fusion.8), channel_id=1, replica_groups=mesh['row'=8,'col'=32] {'row','col'}, use_global_device_ids=true, to_apply=%region_35.38 | all-reduce | flops 1 | bytes 8 | tf_op jit(solution)/shard_map/psum | solution.py:153
  1404.7 73.5 %psum.114 = f32[]{:T(128)} all-reduce(f32[]{:T(128)} %get-tuple-element.404), channel_id=1, replica_groups=mesh['row'=8,'col'=32] {'row','col'}, use_global_device_ids=true, to_apply=%region_37.40 | all-reduce | flops 1 | bytes 8 | tf_op jit(solution)/shard_map/psum | solution.py:145
  1479.1 23.7 %all-gather.5 = f32[32,16,3]{1,2,0:T(4,128)S(1)} all-gather(f32[1,16,3]{1,2,0:T(4,128)S(1)} %bitcast.278), channel_id=1, replica_groups=mesh['row'=8,'col'=32] {'col'}, dimensions={0}, use_global_device_ids=true | all-gather | bytes 6336 | tf_op jit(solution)/shard_map/all_gather | solution.py:134
  1505.3 4.3 all-to-all-start.5
  1516.9 9.3 fusion.115
  1526.4 18.2 reduce-scatter.22.cloned.1.call-done
  1546.1 80.3 %psum.115 = f32[]{:T(128)} all-reduce(f32[]{:T(128)} %get-tuple-element.400), channel_id=1, replica_groups=mesh['row'=8,'col'=32] {'row','col'}, use_global_device_ids=true, to_apply=%region_44.47 | all-reduce | flops 1 | bytes 8 | tf_op jit(solution)/shard_map/psum | solution.py:153
  1627.8 73.4 %psum.116 = f32[]{:T(128)} all-reduce(f32[]{:T(128)} %multiply_reduce_fusion.4), channel_id=1, replica_groups=mesh['row'=8,'col'=32] {'row','col'}, use_global_device_ids=true, to_apply=%region_46.49 | all-reduce | flops 1 | bytes 8 | tf_op jit(solution)/shard_map/psum | solution.py:153
  1703.0 74.2 %psum.117 = f32[]{:T(128)} all-reduce(f32[]{:T(128)} %get-tuple-element.398), channel_id=1, replica_groups=mesh['row'=8,'col'=32] {'row','col'}, use_global_device_ids=true, to_apply=%region_48.51 | all-reduce | flops 1 | bytes 8 | tf_op jit(solution)/shard_map/psum | solution.py:153
  1780.2 73.4 %psum.118 = f32[]{:T(128)} all-reduce(f32[]{:T(128)} %multiply_reduce_fusion.2), channel_id=1, replica_groups=mesh['row'=8,'col'=32] {'row','col'}, use_global_device_ids=true, to_apply=%region_50.53 | all-reduce | flops 1 | bytes 8 | tf_op jit(solution)/shard_map/psum | solution.py:153
  1858.7 74.3 %psum.119 = f32[]{:T(128)} all-reduce(f32[]{:T(128)} %multiply_reduce_fusion.1), channel_id=1, replica_groups=mesh['row'=8,'col'=32] {'row','col'}, use_global_device_ids=true, to_apply=%region_52.55 | all-reduce | flops 1 | bytes 8 | tf_op jit(solution)/shard_map/psum | solution.py:145
  1977.1 4.6 all-to-all-start.6
  1981.8 24.5 %all-gather.6 = f32[32,16,3]{1,2,0:T(4,128)S(1)} all-gather(f32[1,16,3]{1,2,0:T(4,128)S(1)} %bitcast.279), channel_id=1, replica_groups=mesh['row'=8,'col'=32] {'col'}, dimensions={0}, use_global_device_ids=true | all-gather | bytes 6336 | tf_op jit(solution)/shard_map/all_gather | solution.py:134
  2008.3 9.3 fusion.116
  2017.8 18.3 reduce-scatter.24.cloned.1.call-done
  (207 shorter events, 95.2 us)
Async XLA Ops:
  12.7 196.2 %all-to-all-start = ((s32[32,2,1]{1,2,0:T(1,128)}), s32[32,2,1]{1,2,0:T(1,128)S(1)}, u32[]{:S(2)}, u32[]{:S(2)}) async-start(s32[32,2,1]{1,2,0:T(1,128)} %bitcast.5), calls=%async_computation | async-start | bytes 32768 | tf_op jit(solution)/shard_map/all_to_all | solution.py:110
  146.8 21.7 %copy-start = (f32[3,16,128]{2,1,0:T(8,128)S(1)}, f32[3,16,128]{2,1,0:T(8,128)}, u32[]{:S(2)}) copy-start(f32[3,16,128]{2,1,0:T(8,128)} %param.61) | copy-start | bytes 73732
  146.8 21.7 %copy-start.1 = (f32[128]{0:T(128)S(1)}, f32[128]{0:T(128)}, u32[]{:S(2)}) copy-start(f32[128]{0:T(128)} %param.64) | copy-start | bytes 1540
  208.8 28.3 %all-to-all-start.2 = ((bf16[32,2,384]{2,1,0:T(2,128)(2,1)}), bf16[32,2,384]{2,1,0:T(2,128)(2,1)S(1)}, u32[]{:S(2)}, u32[]{:S(2)}) async-start(bf16[32,2,384]{2,1,0:T(2,128)(2,1)} %all_to_all.50), calls=%async_computation.2 | async-start | bytes 98304 | tf_op jit(solution)/shard_map/all_to_all | solution.py:119
  237.1 7.6 copy-start.4
  237.1 376.7 %copy-start.5 = (s32[2]{0:T(128)S(1)}, s32[2]{0:T(128)}, u32[]{:S(2)}) copy-start(s32[2]{0:T(128)} %constant.722.clone.1) | copy-start | bytes 28
  237.2 378.7 %all-to-all-start.1 = ((bf16[32,2,147456]{2,1,0:T(2,128)(2,1)}), bf16[32,2,147456]{2,1,0:T(2,128)(2,1)}, u32[]{:S(2)}, u32[]{:S(2)}) async-start(bf16[32,2,147456]{2,1,0:T(2,128)(2,1)} %broadcast_select_fusion.1), calls=%async_computation.1 | async-start | bytes 37748736 | tf_op jit(solution)/shard_map/all_to_all | solution.py:109
  244.7 410.2 %reduce-scatter.16.cloned.1.call-start = ((), (), s32[]{:S(2)}) async-start(), calls=%async_computation.12 | async-start | bytes 73728
  645.4 9.5 copy-start.2
  645.4 9.5 copy-start.3
  832.7 11.6 all-to-all-start.3
  837.0 33.2 %reduce-scatter.18.cloned.1.call-start = ((), (), s32[]{:S(2)}) async-start(), calls=%async_computation.13 | async-start | bytes 73728
  1129.9 11.6 all-to-all-start.4
  1134.2 33.2 %reduce-scatter.20.cloned.1.call-start = ((), (), s32[]{:S(2)}) async-start(), calls=%async_computation.14 | async-start | bytes 73728
  1505.3 11.6 all-to-all-start.5
  1509.5 35.1 %reduce-scatter.22.cloned.1.call-start = ((), (), s32[]{:S(2)}) async-start(), calls=%async_computation.15 | async-start | bytes 73728
  1977.1 31.2 %all-to-all-start.6 = ((bf16[32,2,384]{2,1,0:T(2,128)(2,1)}), bf16[32,2,384]{2,1,0:T(2,128)(2,1)S(1)}, u32[]{:S(2)}, u32[]{:S(2)}) async-start(bf16[32,2,384]{2,1,0:T(2,128)(2,1)} %all_to_all.62), calls=%async_computation.6 | async-start | bytes 98304 | tf_op jit(solution)/shard_map/all_to_all | solution.py:119
  1981.7 54.5 %reduce-scatter.24.cloned.1.call-start = ((), (), s32[]{:S(2)}) async-start(), calls=%async_computation.16 | async-start | bytes 73728
Sparse Core Ops, SparseCore 0:
  610.8 26.8 reduce-scatter.15
  840.5 29.6 reduce-scatter.17
  1137.5 29.8 reduce-scatter.19
  1514.1 30.4 reduce-scatter.21
  2008.4 27.6 reduce-scatter.23
where the time goes:
time: 2060 us; the launch traced here: 2040 us
  blocking collectives  1590 us (77%)
  local copies, waits for them, and re-layouts  158 us (8%)
  other arithmetic  89.7 us (4%)
  waiting for transfers between devices  79.8 us (4%)
  matrix products  47.3 us (2%)
  between operations  39.6 us (2%)
  starting transfers between devices  38.2 us (2%)
    psum x10, blocking collectives, on_device(): height = lax.psum(jnp.sum(basis[earlier] * image), ('row', 'col'))  757 us
    psum x5, blocking collectives, norm_of(): lax.psum(jnp.sum(vector * vector), ('row', 'col')) + EPSILON  376 us
    all_gather x1, blocking collectives, on_device(): source_pos = lax.all_gather(positions, 'col', axis=1, tiled=True)  318 us
    all_gather x5, blocking collectives, far_field(): lax.all_gather(strengths, 'col', axis=1, tiled=True)  126 us
    gather x4, local copies, waits for them, and re-layouts, on_device(): jnp.take(flat_blocks, anchor, axis=0)  69.5 us
    unnamed x10, waiting for transfers between devices  69.3 us
    dot_general x5, matrix products, near_field(): jnp.einsum('kij,kj->ki', received_blocks, incoming, preferred_element_typ...  46.5 us
  transfers between devices with their start and end apart: 12, of which 7 were waited for; matrix products, arithmetic and copies ran while one was open for 11% of the time, Pallas kernels for 0%

commit v1 on v0

v1 whole, which is shorter than its diff:
```python
import functools
import jax
import jax.numpy as jnp
from jax import lax
from jax.experimental import pallas as pl
from jax.experimental.pallas import tpu as pltpu
from jax.sharding import PartitionSpec as P

CAPD = 2
ITERS = 4
EPSILON = 1e-06
F32 = jnp.float32
BF16 = jnp.bfloat16
HIGHEST = lax.Precision.HIGHEST
LANES = 128
GRAM = {(j, l): l * (l + 1) // 2 + j for l in range(ITERS) for j in range(l + 1)}
HESS = {(j, k): 16 + 8 * k + j for k in range(ITERS) for j in range(k + 2)}
BETA = 63
SHIFT = 2.0


def lane_iota(shape):
    return lax.broadcasted_iota(jnp.int32, shape, len(shape) - 1)


def column(row, size):
    eye = lax.broadcasted_iota(jnp.int32, (size, size), 0) == lane_iota((size, size))
    return jnp.sum(jnp.where(eye, row, 0.0), axis=1, keepdims=True)


def tall(col, comps):
    return jnp.concatenate([col] * comps, axis=0)


def bend(x, stiff):
    points = x.shape[1]
    lane = lane_iota(x.shape)

    def shifted(by):
        moved = pltpu.roll(x, by % points, 1)
        keep = lane >= by if by > 0 else lane < points + by
        return jnp.where(keep, moved, 0.0)

    fourth = shifted(2) - 4.0 * shifted(1) + 6.0 * x - 4.0 * shifted(-1) + shifted(-2)
    return x + stiff * fourth


def placed(x, weights, place, comps, cil):
    sums = jnp.sum(x * weights, axis=1, keepdims=True)
    return [
        jnp.sum(sums[i * cil:(i + 1) * cil] * place, axis=0, keepdims=True) for i in range(comps)
    ]


def place_of(cil):
    shape = (cil, LANES)
    own = lax.axis_index("row") * cil + lax.broadcasted_iota(jnp.int32, shape, 0)
    return jnp.where(lane_iota(shape) == own, 1.0, 0.0)


def to_every(send_ref, parts):
    rows = list(parts)
    rows += [jnp.zeros((1, LANES), F32)] * (send_ref.shape[1] - len(rows))
    tile = jnp.concatenate(rows, axis=0)
    send_ref[...] = jnp.broadcast_to(tile[None], send_ref.shape)


def dot_row(pairs):
    rows = [jnp.sum(a * b, axis=0, keepdims=True) for a, b in pairs]
    while len(rows) % 8:
        rows.append(jnp.zeros_like(rows[0]))
    sums = jnp.sum(jnp.concatenate(rows, axis=0), axis=1, keepdims=True)
    shape = (len(rows), LANES)
    eye = lax.broadcasted_iota(jnp.int32, shape, 0) == lane_iota(shape)
    return jnp.sum(jnp.where(eye, sums, 0.0), axis=0, keepdims=True)


def pick(row, lane):
    return row[:, lane:lane + 1]


def pack(entries):
    lane = lane_iota((1, LANES))
    row = jnp.zeros((1, LANES), F32)
    for where, value in entries.items():
        row = jnp.where(lane == where, value, row)
    return row


def first_kernel(comps, cil, f_ref, pos_ref, w_ref, send_ref):
    f = f_ref[...]
    place = place_of(cil)
    parts = placed(f, w_ref[...], place, comps, cil)
    parts.append(dot_row([(f, f)]))
    for i in range(comps):
        col = column(pos_ref[i:i + 1, :], cil)
        parts.append(jnp.sum(col * place, axis=0, keepdims=True))
    to_every(send_ref, parts)


TILE = 8
META = 6
DOTS = 14
PITCH = {True: 24, False: 16}


def near_kernel(comps, cil, chunk, first, cilia_ref, dest_ref, count_ref, x_ref, b_ref, out_ref,
                lhs, result, used, held, sems):
    points = x_ref.shape[1]
    slots = b_ref.shape[0]

    def fetch(at):
        part = pl.ds(at * chunk, chunk)
        return pltpu.make_async_copy(b_ref.at[part], held.at[part], sems.at[at])

    for at in range(slots // chunk):
        fetch(at).start()
    result[...] = jnp.zeros_like(result)

    def clear(i, carry):
        used[i] = 0
        return carry

    lax.fori_loop(0, used.shape[0], clear, 0)
    x = x_ref[...]
    high = x.astype(BF16).astype(F32)
    low = x - high
    row = lax.broadcasted_iota(jnp.int32, (TILE, points), 0)
    for g in range(cil):
        for i in range(comps):
            at = i * cil + g
            value = jnp.where(row == 0, high[at:at + 1], jnp.where(row == 1, low[at:at + 1], 0.0))
            lhs[g, :, i * points:(i + 1) * points] = value.astype(BF16)
    lane = lane_iota((1, points))
    for at in range(slots // chunk):
        fetch(at).wait()
        speeds = [
            lax.dot_general(
                lhs[cilia_ref[0, slot]], held[slot], (((1,), (1,)), ((), ())),
                preferred_element_type=F32,
            )
            for slot in range(at * chunk, (at + 1) * chunk)
        ]
        for s in range(chunk):
            slot = at * chunk + s
            dest = dest_ref[slot]
            rank = used[dest]
            used[dest] = rank + 1
            live = slot < count_ref[0]
            speed = jnp.where(live, speeds[s][0:1] + speeds[s][1:2], 0.0)
            for i in range(comps):
                result[dest, pl.ds(rank * comps + i, 1), :] = speed[:, i * points:(i + 1) * points]
            if first:
                target = cilia_ref[1, slot].astype(F32)
                before = result[dest, META:META + 1, :]
                result[dest, META:META + 1, :] = jnp.where(lane == rank, target, before)
    out_ref[...] = result[...].astype(BF16)


def join_kernel(comps, first, rows_ref, near_ref, send_ref):
    total = jnp.sum(rows_ref[...], axis=0)
    high = total.astype(BF16).astype(F32)
    rest = total - high
    middle = rest.astype(BF16).astype(F32)
    low = rest - middle
    at = comps
    shared = jnp.concatenate(
        [
            high[:at], rest[:at], high[at:at + 1],
            middle[at:at + 1] + pltpu.roll(low[at:at + 1], LANES // 2, 1),
        ],
        axis=0,
    )
    send_ref[:, :TILE, :] = near_ref[...]
    send_ref[:, TILE:2 * TILE, :] = jnp.broadcast_to(
        shared.astype(BF16)[None], (send_ref.shape[0],) + shared.shape
    )
    if first:
        at = comps + 1
        places = jnp.concatenate(
            [high[at:at + comps], rest[at:at + comps], jnp.zeros((TILE - 2 * comps, LANES), F32)], axis=0
        )
        send_ref[:, 2 * TILE:3 * TILE, :] = jnp.broadcast_to(
            places.astype(BF16)[None], (send_ref.shape[0],) + places.shape
        )


def sorting(comps, cil, sources, pitch, targets):
    def parts(rows):
        shape = (rows, sources * pitch)
        row = lax.broadcasted_iota(jnp.int32, shape, 0)
        lane = lane_iota(shape)
        return row, lax.div(lane, pitch), lax.rem(lane, pitch)

    row, _, place = parts(comps * cil)
    comp, cilium = lax.div(row, cil), lax.rem(row, cil).astype(F32)
    found = jnp.zeros(row.shape, jnp.bool_)
    for rank in range(CAPD):
        found |= (place == rank * comps + comp) & (cilium == targets[rank])
    pieces = [found]

    def gathered(start):
        row, source, place = parts(comps * sources)
        comp, wanted = lax.div(row, sources), lax.rem(row, sources)
        here = (place == start + comp) | (place == start + comps + comp)
        return here & (source == wanted)

    pieces.append(gathered(TILE))
    row, _, place = parts(TILE)
    pieces.append((row == 0) & ((place == DOTS) | (place == DOTS + 1)))
    if pitch > 2 * TILE:
        pieces.append(gathered(2 * TILE))
    return jnp.concatenate([jnp.where(p, 1.0, 0.0) for p in pieces], axis=0).astype(BF16)


def applied(x, stiff, rows, pairs, profile, comps, cil, sources):
    flat = comps * cil
    image = bend(x, stiff) + rows[:flat]
    totals = [jnp.zeros((cil, LANES), F32) for _ in range(comps)]
    for s in range(sources):
        strength = [rows[flat + j * sources + s:flat + j * sources + s + 1] for j in range(comps)]
        for (i, j), at in PAIRS.items():
            block = pairs(at, s)
            totals[i] = totals[i] + block * strength[j]
            if i != j:
                totals[j] = totals[j] + block * strength[i]
    far = jnp.concatenate([jnp.sum(t, axis=1, keepdims=True) for t in totals], axis=0)
    dots = rows[flat + comps * sources:flat + comps * sources + 1]
    dots = dots + pltpu.roll(dots, LANES // 2, 1)
    return image + far * profile, dots


PAIRS = {(0, 0): 0, (0, 1): 1, (0, 2): 2, (1, 1): 3, (1, 2): 4, (2, 2): 5}


def krylov_kernel(comps, cil, sources, total, step, *refs):
    first = step == 1
    last = step == ITERS
    refs = list(refs)
    recv_ref, x_ref, stiff_ref, prof_ref = refs[:4]
    refs = refs[4:]
    if not last:
        w_ref = refs.pop(0)
    if first:
        pos_ref = refs.pop(0)
    else:
        sort_ref, pairs_ref, state_ref, v_ref, z_ref = refs[:5]
        refs = refs[5:]
    if first:
        sort_out, pairs_out = refs[:2]
        refs = refs[2:]
    send_ref, x_out, v_out, z_out, state_out, rows = refs
    x = x_ref[...]
    flat = comps * cil
    stiff = tall(column(stiff_ref[...], cil), comps)

    if first:
        pitch = PITCH[True]
        arrived = recv_ref[...]
        shape = (sources, sources * pitch)
        source, lane = lax.broadcasted_iota(jnp.int32, shape, 0), lane_iota(shape)
        chosen = jnp.where(lane == source * pitch + META, 1.0, 0.0).astype(BF16)
        meta = jnp.dot(chosen, arrived, preferred_element_type=F32)
        eye = lax.broadcasted_iota(jnp.int32, (sources, sources), 0) == lane_iota((sources, sources))
        named = [
            jnp.sum(jnp.where(eye, pick(meta, rank), 0.0), axis=0, keepdims=True) for rank in range(CAPD)
        ]
        named = jnp.concatenate(
            [jnp.broadcast_to(n, (TILE, sources)) for n in named], axis=0
        ).astype(BF16)

        def targets_for(pitch):
            shape = (sources, sources * pitch)
            source, lane = lax.broadcasted_iota(jnp.int32, shape, 0), lane_iota(shape)
            spread = jnp.where(lax.div(lane, pitch) == source, 1.0, 0.0).astype(BF16)
            wide = jnp.dot(named, spread, preferred_element_type=F32)
            return [wide[rank * TILE:rank * TILE + 1] for rank in range(CAPD)]

        sort_out[...] = sorting(comps, cil, sources, PITCH[False], targets_for(PITCH[False]))
        sort = sorting(comps, cil, sources, pitch, targets_for(pitch))
        rows[...] = jnp.dot(sort, arrived, preferred_element_type=F32)
        eps_three = 4.0 / total
        eps_two = eps_three ** (2.0 / 3.0)
        here = [
            jnp.broadcast_to(column(pos_ref[i:i + 1, :], cil), (cil, LANES)) for i in range(comps)
        ]
        start = flat + comps * sources + TILE
        for s in range(sources):
            gap = [
                here[i] - rows[start + i * sources + s:start + i * sources + s + 1]
                for i in range(comps)
            ]
            inverse = 1.0 / (gap[0] * gap[0] + gap[1] * gap[1] + gap[2] * gap[2] + eps_two)
            amplitude = eps_three * inverse * jnp.sqrt(inverse)
            slope = amplitude * inverse
            for (i, j), at in PAIRS.items():
                block = slope * gap[i] * gap[j]
                pairs_out[at, s] = block + amplitude if i == j else block
        pairs = lambda at, s: pairs_out[at, s]
    else:
        rows[...] = jnp.dot(sort_ref[...], recv_ref[...], preferred_element_type=F32)
        pairs = lambda at, s: pairs_ref[at, s]

    image, dots = applied(x, stiff, rows, pairs, prof_ref[...], comps, cil, sources)
    entries = {}
    if first:
        beta = jnp.sqrt(pick(dots, 0) + EPSILON)
        entries[BETA] = beta
        scale = 1.0 / beta
        basis = [x * scale]
        images = [image * scale]
    else:
        state = state_ref[...]
        count = step - 1
        gram, products, square = read_dots(dots, state, count)
        basis = [v_ref[j] for j in range(count)]
        images = [z_ref[j] for j in range(count)]
        heights, taken, length = heights_of(gram, products, square, shifts_of(count), count)
        scale = 1.0 / length
        vector, product = x, image
        for j in range(count):
            vector = vector - taken[j] * basis[j]
            product = product - taken[j] * images[j]
        basis.append(vector * scale)
        images.append(product * scale)
        for j in range(count):
            entries[GRAM[j, count - 1]] = gram[j, count - 1]
            entries[HESS[j, count - 1]] = heights[j]
        entries[HESS[count, count - 1]] = length
    row = pack(entries)
    state_out[...] = row if first else row + state
    for j in range(step):
        v_out[j] = basis[j]
        z_out[j] = images[j]
    outgoing = images[-1]
    for j, shift in enumerate(shifts_of(step)):
        if shift:
            outgoing = outgoing - shift * basis[j]
    pairs_of_dots = [(basis[j], basis[-1]) for j in range(step)]
    pairs_of_dots += [(basis[j], outgoing) for j in range(step)]
    pairs_of_dots.append((outgoing, outgoing))
    local = dot_row(pairs_of_dots)
    if last:
        to_every(send_ref, [local])
    else:
        to_every(send_ref, placed(outgoing, w_ref[...], place_of(cil), comps, cil) + [local])
    x_out[...] = outgoing


def shifts_of(count):
    if count == ITERS:
        return [0.0] * count
    return [0.0] * (count - 1) + [SHIFT]


def read_dots(dots, state, count):
    gram = {}
    for l in range(count):
        for j in range(l + 1):
            gram[j, l] = pick(dots, j) if l == count - 1 else pick(state, GRAM[j, l])
            gram[l, j] = gram[j, l]
    return gram, [pick(dots, count + j) for j in range(count)], pick(dots, 2 * count)


def heights_of(gram, products, square, shifts, count):
    heights, taken = [], []
    for j in range(count):
        extra = sum((shifts[l] * gram[j, l] for l in range(count) if shifts[l]), 0.0)
        heights.append(products[j] + extra)
        taken.append(heights[j] - shifts[j])
    norm = square
    for j in range(count):
        inner = -2.0 * products[j]
        for l in range(count):
            inner = inner + taken[l] * gram[j, l]
        norm = norm + taken[j] * inner
    return heights, taken, jnp.sqrt(jnp.maximum(norm, 0.0) + EPSILON)


def solve_kernel(rows_ref, state_ref, f_ref, v_ref, z_ref, solution_ref, residual_ref):
    dots = jnp.sum(rows_ref[...], axis=0)
    state = state_ref[...]
    gram, products, square = read_dots(dots, state, ITERS)
    heights, _, length = heights_of(gram, products, square, shifts_of(ITERS), ITERS)
    zero = jnp.zeros((1, 1), F32)
    columns = []
    for k in range(ITERS):
        if k == ITERS - 1:
            entries = heights + [length]
        else:
            entries = [pick(state, HESS[j, k]) for j in range(k + 2)]
        columns.append(entries + [zero] * (ITERS + 1 - len(entries)))
    units, triangle = [], {}
    for k in range(ITERS):
        vector = columns[k]
        for e in range(k):
            used = min(e + 2, k + 2)
            weight = sum(units[e][j] * vector[j] for j in range(used))
            triangle[e, k] = weight
            vector = [vector[j] - weight * units[e][j] if j < used else vector[j] for j in range(ITERS + 1)]
        size = jnp.sqrt(sum(vector[j] * vector[j] for j in range(k + 2)))
        triangle[k, k] = size
        units.append([vector[j] / size for j in range(ITERS + 1)])
    beta = pick(state, BETA)
    answers = [None] * ITERS
    for k in reversed(range(ITERS)):
        running = beta * units[k][0]
        for later in range(k + 1, ITERS):
            running = running - triangle[k, later] * answers[later]
        answers[k] = running / triangle[k, k]
    result = answers[0] * v_ref[0]
    rest = f_ref[...] - answers[0] * z_ref[0]
    for k in range(1, ITERS):
        result = result + answers[k] * v_ref[k]
        rest = rest - answers[k] * z_ref[k]
    solution_ref[...] = result
    residual_ref[...] = rest


def on_device(
    forcing,
    stiffness,
    positions,
    far_weights,
    far_profile,
    near_blocks,
    near_dest,
    near_cilia,
    near_count,
):
    rows = lax.axis_size("row")
    cols = lax.axis_size("col")
    comps, cil, points = forcing.shape
    slots = near_blocks.shape[0]
    width = comps * points
    flat = comps * cil
    total = cil * rows * cols
    chunk = 4
    struct = lambda *shape, dtype=F32: jax.ShapeDtypeStruct(shape, dtype)
    vmem, smem = pl.BlockSpec(memory_space=pltpu.VMEM), pl.BlockSpec(memory_space=pltpu.SMEM)
    slim = pltpu.CompilerParams(vmem_limit_bytes=4 << 20)
    roomy = pltpu.CompilerParams(vmem_limit_bytes=8 << 20)
    f = forcing.reshape(flat, points)
    stiff = stiffness.reshape(1, cil)
    weights = far_weights.reshape(1, points)
    profile = far_profile.reshape(1, points)
    cilia = near_cilia.T
    dest = near_dest.reshape(slots)

    blocks = pltpu.with_memory_space_constraint(near_blocks, pltpu.HBM)

    def exchange(send, x, first):
        arrived = lax.all_to_all(send, "row", split_axis=0, concat_axis=0, tiled=True)
        near = pl.pallas_call(
            functools.partial(near_kernel, comps, cil, chunk, first),
            out_shape=struct(cols, TILE, LANES, dtype=BF16),
            in_specs=[smem, smem, smem, vmem, pl.BlockSpec(memory_space=pltpu.HBM)],
            out_specs=vmem,
            scratch_shapes=[
                pltpu.VMEM((cil, TILE, width), BF16),
                pltpu.VMEM((cols, TILE, points), F32),
                pltpu.SMEM((cols,), jnp.int32),
                pltpu.VMEM(blocks.shape, BF16),
                pltpu.SemaphoreType.DMA((slots // chunk,)),
            ],
            compiler_params=pltpu.CompilerParams(vmem_limit_bytes=16 << 20),
            name="near",
        )(cilia, dest, near_count, x, blocks)
        out = pl.pallas_call(
            functools.partial(join_kernel, comps, first),
            out_shape=struct(cols, PITCH[first], LANES, dtype=BF16),
            compiler_params=slim,
            name="join",
        )(arrived, near)
        recv = lax.all_to_all(out, "col", split_axis=0, concat_axis=0, tiled=True)
        return recv.reshape(cols * PITCH[first], LANES)

    send = pl.pallas_call(
        functools.partial(first_kernel, comps, cil),
        out_shape=struct(rows, TILE, LANES),
        compiler_params=slim,
        name="first",
    )(f, positions, weights)
    recv = exchange(send, f, True)
    x = f
    sorted_rows = flat + comps * cols + TILE
    for step in range(1, ITERS + 1):
        first, last = step == 1, step == ITERS
        ins = [recv, x, stiff, profile]
        if not last:
            ins.append(weights)
        ins += [positions] if first else [sort, pairs, state, vs, zs]
        outs = []
        if first:
            outs += [
                struct(sorted_rows, cols * PITCH[False], dtype=BF16),
                struct(len(PAIRS), cols, cil, LANES),
            ]
        outs += [
            struct(rows * cols if last else rows, 1 if last else TILE, LANES),
            struct(flat, points),
            struct(step, flat, points),
            struct(step, flat, points),
            struct(1, LANES),
        ]
        results = pl.pallas_call(
            functools.partial(krylov_kernel, comps, cil, cols, total, step),
            out_shape=outs,
            scratch_shapes=[pltpu.VMEM((sorted_rows + comps * cols * first, LANES), F32)],
            compiler_params=roomy,
            name="krylov",
        )(*ins)
        if first:
            sort, pairs = results[:2]
            results = results[2:]
        send, x, vs, zs, state = results
        if not last:
            recv = exchange(send, x, False)
    everyone = lax.all_to_all(send, ("row", "col"), split_axis=0, concat_axis=0, tiled=True)
    out, rest = pl.pallas_call(
        solve_kernel, out_shape=[struct(flat, points)] * 2, compiler_params=slim, name="solve"
    )(everyone, state, f, vs, zs)
    return out.reshape(forcing.shape), rest.reshape(forcing.shape)


def solution(mesh):
    in_specs = (
        P(None, ("row", "col"), None),
        P(("row", "col")),
        P(None, ("row", "col")),
        P(),
        P(),
        P(("row", "col"), None, None),
        P(("row", "col"), None),
        P(("row", "col"), None),
        P(("row", "col")),
    )
    out_specs = (P(None, ("row", "col"), None), P(None, ("row", "col"), None))
    return jax.shard_map(
        on_device, mesh=mesh, in_specs=in_specs, out_specs=out_specs, check_vma=False
    )
```

time: 2060 us -> 141 us (0.07)
  blocking collectives: 1590 us -> 74 us
  local copies, waits for them, and re-layouts: 158 us -> 4.19 us
  other arithmetic: 89.7 us -> 0 us
  waiting for transfers between devices: 79.8 us -> 4.08 us
  matrix products: 47.3 us -> 0 us
  between operations: 39.6 us -> 1.43 us
  Pallas kernels: 0 us -> 31.6 us
    psum x15 -> x0, blocking collectives: 1130 us -> none  [the longest x10 757 us: on_device(): height = lax.psum(jnp.sum(basis[earlier] * image), ('row', 'col'))]
    all_gather x7 -> x0, blocking collectives: 459 us -> none  [the longest x1 318 us: on_device(): source_pos = lax.all_gather(positions, 'col', axis=1, tiled=True)]
    gather x16 -> x0, local copies, waits for them, and re-layouts: 77 us -> none  [the longest x4 69.5 us: on_device(): jnp.take(flat_blocks, anchor, axis=0)]
    all_to_all x0 -> x5, blocking collectives: none -> 74 us  [the longest x4 54.1 us: exchange(): recv = lax.all_to_all(out, 'col', split_axis=0, concat_axis=0, tiled=True)]
    unnamed x10 -> x0, waiting for transfers between devices: 69.3 us -> none
    dot_general x10 -> x0, matrix products: 47.3 us -> none  [the longest x5 46.5 us: near_field(): jnp.einsum('kij,kj->ki', received_blocks, incoming, preferred_element_typ...]
    reduce_sum x39 -> x0, other arithmetic: 38.1 us -> none  [the longest x10 14.8 us: on_device(): height = lax.psum(jnp.sum(basis[earlier] * image), ('row', 'col'))]
    pallas_call x0 -> x14, Pallas kernels: none -> 31.6 us  [the longest x4 22.3 us: exchange(): pl.pallas_call(functools.partial(near_kernel, comps, cil, chunk, first),...]
  transfers between devices with their start and end apart: 12 -> 4, of which waited for: 7 -> 3; matrix products, arithmetic and copies ran while one was open for 11% -> 0% of each run, Pallas kernels for 0% -> 16%
where the time goes in v1:
time: 141 us; the launch traced here: 140 us
  blocking collectives  74 us (52%)
  Pallas kernels  31.6 us (22%)
  starting transfers between devices  24.9 us (18%)
  local copies, waits for them, and re-layouts  4.19 us (3%)
  waiting for transfers between devices  4.08 us (3%)
  between operations  1.43 us (1%)
    all_to_all x4, blocking collectives, exchange(): recv = lax.all_to_all(out, 'col', split_axis=0, concat_axis=0, tiled=True)  54.1 us
    all_to_all x4, starting transfers between devices, exchange(): lax.all_to_all(send, 'row', split_axis=0, concat_axis=0, tiled=True)  24.9 us
    pallas_call x4, Pallas kernels, exchange(): pl.pallas_call(functools.partial(near_kernel, comps, cil, chunk, first),...  22.3 us
    all_to_all x1, blocking collectives, on_device(): lax.all_to_all(send, ('row', 'col'), split_axis=0, concat_axis=0, tiled=T...  19.9 us
    pallas_call x4, Pallas kernels, on_device(): pl.pallas_call(functools.partial(krylov_kernel, comps, cil, cols, total,...  5.99 us
    unnamed x26, local copies, waits for them, and re-layouts  4.19 us
    all_to_all x4, waiting for transfers between devices, exchange(): lax.all_to_all(send, 'row', split_axis=0, concat_axis=0, tiled=True)  4.08 us
  transfers between devices with their start and end apart: 4, of which 3 were waited for; matrix products, arithmetic and copies ran while one was open for 0% of the time, Pallas kernels for 16%

profile of v1, /device:TPU:1, one launch (start us, length us, event | category | flops | bytes accessed | tf_op | source)
XLA Modules:
  0.0 140.2 jit_solution(8085912167946086112)
XLA Ops:
  0.6 0.0 copy-start.6
  0.6 0.0 copy-start.4
  0.7 0.0 copy-start.8
  0.7 0.0 copy-start.12
  0.7 0.0 copy-start.11
  0.7 0.0 copy-start
  0.7 0.8 copy-done
  1.4 0.0 copy-start.5
  1.5 0.7 copy-done.5
  2.1 0.7 copy-done.9
  2.8 0.7 first.1
  3.5 9.0 %all-to-all-start = ((f32[8,8,128]{2,1,0:T(8,128)}), f32[8,8,128]{2,1,0:T(8,128)S(1)}, u32[]{:S(2)}, u32[]{:S(2)}) async-start(f32[8,8,128]{2,1,0:T(8,128)} %first.1), calls=%async_computation | async-start | bytes 65536 | tf_op jit(solution)/shard_map/all_to_all | solution.py:453
  13.2 0.0 copy-start.1
  13.2 0.7 copy-done.1
  13.9 0.7 copy-done.3
  14.6 0.7 copy-done.7
  15.2 5.6 %near.4.near_ref = bf16[32,8,128]{2,1,0:T(8,128)(2,1)S(1)} custom-call(s32[2,32]{1,0:T(2,128)S(1)} %bitcast.20, s32[32]{0:T(128)S(1)} %bitcast.28, s32[1]{0:T(128)S(6)} %copy.11.count_ref, f32[48,128]{1,0:T(8,128)S(1)} %bitcast.17, bf16[32,384,384]{2,1,0:T(8,128)(2,1)} %b_ref.7), custom_call_target="tpu_custom_call" | custom-call | tf_op jit(solution)/shard_map/near/pallas_call | solution.py:454
  20.8 0.0 all-to-all-done.rows_ref
  20.8 0.1 join.4
  20.9 16.2 %all_to_all.45 = bf16[32,24,128]{2,1,0:T(8,128)(2,1)S(1)} all-to-all(bf16[32,24,128]{2,1,0:T(8,128)(2,1)S(1)} %join.4), channel_id=1, replica_groups=mesh['row'=8,'col'=32] {'col'}, dimensions={0} | all-to-all | bytes 393216 | tf_op jit(solution)/shard_map/all_to_all | solution.py:475
  37.1 0.0 copy-done.6
  37.1 0.0 copy-done.12
  37.1 0.0 copy-done.11
  37.1 0.0 copy-done.2
  37.1 0.0 copy-done.10
  37.1 2.1 %krylov.4 = (bf16[152,512]{1,0:T(8,128)(2,1)S(1)}, f32[6,32,16,128]{3,2,1,0:T(8,128)S(1)}, f32[8,8,128]{2,1,0:T(8,128)}, f32[48,128]{1,0:T(8,128)S(1)}, f32[1,48...) custom-call(bf16[768,128]{1,0:T(8,128)(2,1)S(1)} %bitcast.12, f32[48,128]{1,0:T(8,128)S(1)} %bitcast.18, ...), custom_call_target="tpu_custom_call" | custom-call | tf_op jit(solution)/shard_map/krylov/pallas_call | solution.py:506
  39.3 6.9 %all-to-all-start.2 = ((f32[8,8,128]{2,1,0:T(8,128)}), f32[8,8,128]{2,1,0:T(8,128)S(1)}, u32[]{:S(2)}, u32[]{:S(2)}) async-start(f32[8,8,128]{2,1,0:T(8,128)} %get-tuple-element.25), calls=%async_computation.2 | async-start | bytes 65536 | tf_op jit(solution)/shard_map/all_to_all | solution.py:453
  46.2 0.0 copy-done.4
  46.2 0.0 copy-done.8
  46.2 5.6 %near.5.near_ref = bf16[32,8,128]{2,1,0:T(8,128)(2,1)S(1)} custom-call(s32[2,32]{1,0:T(2,128)S(1)} %bitcast.21, s32[32]{0:T(128)S(1)} %bitcast.29, s32[1]{0:T(128)S(6)} %copy.11.count_ref, f32[48,128]{1,0:T(8,128)S(1)} %get-tuple-element.26.x_ref.refs_1_, bf16[32,384,384]{2,1,0:T(8,128)(2,1)} %b_ref.7), custom_call_target="tpu_custom_call" | custom-call | tf_op jit(solution)/shard_map/near/pallas_call | solution.py:454
  51.8 1.3 all-to-all-done.2.rows_ref
  53.1 0.1 join.5
  53.2 12.7 %all_to_all.46 = bf16[32,16,128]{2,1,0:T(8,128)(2,1)S(1)} all-to-all(bf16[32,16,128]{2,1,0:T(8,128)(2,1)S(1)} %join.5), channel_id=1, replica_groups=mesh['row'=8,'col'=32] {'col'}, dimensions={0} | all-to-all | bytes 262144 | tf_op jit(solution)/shard_map/all_to_all | solution.py:475
  65.8 1.3 krylov.5
  67.2 4.5 %all-to-all-start.4 = ((f32[8,8,128]{2,1,0:T(8,128)}), f32[8,8,128]{2,1,0:T(8,128)S(1)}, u32[]{:S(2)}, u32[]{:S(2)}) async-start(f32[8,8,128]{2,1,0:T(8,128)} %get-tuple-element.32), calls=%async_computation.4 | async-start | bytes 65536 | tf_op jit(solution)/shard_map/all_to_all | solution.py:453
  71.7 5.6 %near.6.near_ref = bf16[32,8,128]{2,1,0:T(8,128)(2,1)S(1)} custom-call(s32[2,32]{1,0:T(2,128)S(1)} %bitcast.22, s32[32]{0:T(128)S(1)} %bitcast.30, s32[1]{0:T(128)S(6)} %copy.11.count_ref, f32[48,128]{1,0:T(8,128)S(1)} %get-tuple-element.33.x_ref.refs_1_, bf16[32,384,384]{2,1,0:T(8,128)(2,1)} %b_ref.7), custom_call_target="tpu_custom_call" | custom-call | tf_op jit(solution)/shard_map/near/pallas_call | solution.py:454
  77.3 1.4 all-to-all-done.4.rows_ref
  78.7 0.1 join.6
  78.8 12.6 %all_to_all.47 = bf16[32,16,128]{2,1,0:T(8,128)(2,1)S(1)} all-to-all(bf16[32,16,128]{2,1,0:T(8,128)(2,1)S(1)} %join.6), channel_id=1, replica_groups=mesh['row'=8,'col'=32] {'col'}, dimensions={0} | all-to-all | bytes 262144 | tf_op jit(solution)/shard_map/all_to_all | solution.py:475
  91.4 1.3 krylov.6
  92.7 4.5 %all-to-all-start.6 = ((f32[8,8,128]{2,1,0:T(8,128)}), f32[8,8,128]{2,1,0:T(8,128)S(1)}, u32[]{:S(2)}, u32[]{:S(2)}) async-start(f32[8,8,128]{2,1,0:T(8,128)} %get-tuple-element.37), calls=%async_computation.6 | async-start | bytes 65536 | tf_op jit(solution)/shard_map/all_to_all | solution.py:453
  97.2 5.6 %near.7.near_ref = bf16[32,8,128]{2,1,0:T(8,128)(2,1)S(1)} custom-call(s32[2,32]{1,0:T(2,128)S(1)} %bitcast.23, s32[32]{0:T(128)S(1)} %bitcast.31, s32[1]{0:T(128)S(6)} %copy.11.count_ref, f32[48,128]{1,0:T(8,128)S(1)} %get-tuple-element.38.x_ref.refs_1_, bf16[32,384,384]{2,1,0:T(8,128)(2,1)} %b_ref.7), custom_call_target="tpu_custom_call" | custom-call | tf_op jit(solution)/shard_map/near/pallas_call | solution.py:454
  102.7 1.4 all-to-all-done.6.rows_ref
  104.1 0.1 join.7
  104.2 12.6 %all_to_all.48 = bf16[32,16,128]{2,1,0:T(8,128)(2,1)S(1)} all-to-all(bf16[32,16,128]{2,1,0:T(8,128)(2,1)S(1)} %join.7), channel_id=1, replica_groups=mesh['row'=8,'col'=32] {'col'}, dimensions={0} | all-to-all | bytes 262144 | tf_op jit(solution)/shard_map/all_to_all | solution.py:475
  116.8 1.2 krylov.7
  118.1 19.9 %all_to_all.49.rows_ref = f32[256,1,128]{2,1,0:T(1,128)S(1)} all-to-all(f32[256,1,128]{2,1,0:T(1,128)S(1)} %get-tuple-element.42), channel_id=1, replica_groups=mesh['row'=8,'col'=32] {'row','col'}, dimensions={0} | all-to-all | bytes 262144 | tf_op jit(solution)/shard_map/all_to_all | solution.py:519
  138.0 2.2 %solve.1 = (f32[48,128]{1,0:T(8,128)}, f32[48,128]{1,0:T(8,128)}) custom-call(f32[256,1,128]{2,1,0:T(1,128)S(1)} %all_to_all.49.rows_ref, f32[1,128]{1,0:T(1,128)S(1)} %get-tuple-element.43.state_ref, f32[48,128]{1,0:T(8,128)S(1)} %bitcast.19, f32[4,48,128]{2,1,0:T(8,128)S(1)} %get-tuple-element.44.v_ref, f32[4,48,128]{2,1,0:T(8,128)S(1)} %get-tuple-element.45.z_ref), custom_call_target="tpu_custom_call" | custom-call | tf_op jit(solution)/shard_map/solve/pallas_call | solution.py:520
  (5 shorter events, 0.0 us)
Async XLA Ops:
  0.6 36.5 %copy-start.6 = (f32[128]{0:T(128)S(1)}, f32[128]{0:T(128)}, u32[]{:S(2)}) copy-start(f32[128]{0:T(128)} %param.12) | copy-start | bytes 1540
  0.6 45.6 %copy-start.4 = (s32[32,2]{0,1:T(2,128)S(1)}, s32[32,2]{0,1:T(2,128)}, u32[]{:S(2)}) copy-start(s32[32,2]{0,1:T(2,128)} %param.16) | copy-start | bytes 772
  0.7 45.6 %copy-start.8 = (s32[32,1]{0,1:T(1,128)S(1)}, s32[32,1]{0,1:T(1,128)}, u32[]{:S(2)}) copy-start(s32[32,1]{0,1:T(1,128)} %param.15) | copy-start | bytes 388
  0.7 36.5 %copy-start.12 = (f32[128]{0:T(128)S(1)}, f32[128]{0:T(128)}, u32[]{:S(2)}) copy-start(f32[128]{0:T(128)} %param.13) | copy-start | bytes 1540
  0.7 36.4 %copy-start.11 = (f32[16]{0:T(128)S(1)}, f32[16]{0:T(128)}, u32[]{:S(2)}) copy-start(f32[16]{0:T(128)} %param.10) | copy-start | bytes 196
  0.7 0.8 copy-start
  1.4 0.7 copy-start.5
  2.1 0.7 copy-start.9
  2.8 34.3 %copy-start.2 = (f32[3,16,128]{2,1,0:T(8,128)S(1)}, f32[3,16,128]{2,1,0:T(8,128)}, u32[]{:S(2)}) copy-start(f32[3,16,128]{2,1,0:T(8,128)} %param.9) | copy-start | bytes 73732
  2.8 34.3 %copy-start.10 = (f32[3,16]{1,0:T(4,128)S(1)}, f32[3,16]{1,0:T(4,128)}, u32[]{:S(2)}) copy-start(f32[3,16]{1,0:T(4,128)} %refs_5_.1) | copy-start | bytes 580
  3.5 17.3 %all-to-all-start = ((f32[8,8,128]{2,1,0:T(8,128)}), f32[8,8,128]{2,1,0:T(8,128)S(1)}, u32[]{:S(2)}, u32[]{:S(2)}) async-start(f32[8,8,128]{2,1,0:T(8,128)} %first.1), calls=%async_computation | async-start | bytes 65536 | tf_op jit(solution)/shard_map/all_to_all | solution.py:453
  13.2 0.7 copy-start.1
  13.9 0.7 copy-start.3
  14.6 0.7 copy-start.7
  39.3 13.8 %all-to-all-start.2 = ((f32[8,8,128]{2,1,0:T(8,128)}), f32[8,8,128]{2,1,0:T(8,128)S(1)}, u32[]{:S(2)}, u32[]{:S(2)}) async-start(f32[8,8,128]{2,1,0:T(8,128)} %get-tuple-element.25), calls=%async_computation.2 | async-start | bytes 65536 | tf_op jit(solution)/shard_map/all_to_all | solution.py:453
  67.2 11.5 %all-to-all-start.4 = ((f32[8,8,128]{2,1,0:T(8,128)}), f32[8,8,128]{2,1,0:T(8,128)S(1)}, u32[]{:S(2)}, u32[]{:S(2)}) async-start(f32[8,8,128]{2,1,0:T(8,128)} %get-tuple-element.32), calls=%async_computation.4 | async-start | bytes 65536 | tf_op jit(solution)/shard_map/all_to_all | solution.py:453
  92.7 11.5 %all-to-all-start.6 = ((f32[8,8,128]{2,1,0:T(8,128)}), f32[8,8,128]{2,1,0:T(8,128)S(1)}, u32[]{:S(2)}, u32[]{:S(2)}) async-start(f32[8,8,128]{2,1,0:T(8,128)} %get-tuple-element.37), calls=%async_computation.6 | async-start | bytes 65536 | tf_op jit(solution)/shard_map/all_to_all | solution.py:453

commit v2 on v1

--- a/solution.py
+++ b/solution.py
@@ -16,6 +16,8 @@
 GRAM = {(j, l): l * (l + 1) // 2 + j for l in range(ITERS) for j in range(l + 1)}
 HESS = {(j, k): 16 + 8 * k + j for k in range(ITERS) for j in range(k + 2)}
 BETA = 63
+UPPER = {(e, k): 64 + 4 * k + e for k in range(ITERS) for e in range(k + 1)}
+UNIT = {(k, j): 80 + 8 * k + j for k in range(ITERS) for j in range(k + 2)}
 SHIFT = 2.0
 
 
@@ -59,6 +61,9 @@
 
 
 def to_every(send_ref, parts):
+    if len(send_ref.shape) == 2:
+        send_ref[...] = jnp.broadcast_to(parts[0], send_ref.shape)
+        return
     rows = list(parts)
     rows += [jnp.zeros((1, LANES), F32)] * (send_ref.shape[1] - len(rows))
     tile = jnp.concatenate(rows, axis=0)
@@ -87,9 +92,17 @@
     return row
 
 
-def first_kernel(comps, cil, f_ref, pos_ref, w_ref, send_ref):
-    f = f_ref[...]
+def first_kernel(comps, cil, f_hbm, pos_hbm, w_hbm, send_ref, x_out, pos_ref, w_ref, sems):
+    copies = [
+        pltpu.make_async_copy(source, target, sems.at[n])
+        for n, (source, target) in enumerate(((f_hbm, x_out), (pos_hbm, pos_ref), (w_hbm, w_ref)))
+    ]
+    for copy in copies:
+        copy.start()
     place = place_of(cil)
+    for copy in copies:
+        copy.wait()
+    f = x_out[...]
     parts = placed(f, w_ref[...], place, comps, cil)
     parts.append(dot_row([(f, f)]))
     for i in range(comps):
@@ -99,22 +112,50 @@
 
 
 TILE = 8
+KEPT = 6
 META = 6
 DOTS = 14
 PITCH = {True: 24, False: 16}
 
 
-def near_kernel(comps, cil, chunk, first, cilia_ref, dest_ref, count_ref, x_ref, b_ref, out_ref,
-                lhs, result, used, held, sems):
+def near_kernel(comps, cil, chunk, first, cilia_hbm, dest_hbm, count_ref, x_ref, b_ref, kept_in, *refs):
+    if first:
+        out_ref, kept, lhs, result, used, held, cilia_ref, dest_ref, sems, table_sems = refs
+    else:
+        out_ref, lhs, result, used, held, cilia_ref, dest_ref, sems, table_sems = refs
+        kept = kept_in
     points = x_ref.shape[1]
     slots = b_ref.shape[0]
 
-    def fetch(at):
-        part = pl.ds(at * chunk, chunk)
-        return pltpu.make_async_copy(b_ref.at[part], held.at[part], sems.at[at])
-
+    def block(slot):
+        return kept[slot] if slot < KEPT else held[slot - KEPT]
+
+    def fetches(at):
+        start, stop = at * chunk, (at + 1) * chunk
+        parts = []
+        if first and start < KEPT:
+            parts.append((start, min(stop, KEPT), kept, 0))
+        if stop > KEPT:
+            parts.append((max(start, KEPT), stop, held, KEPT))
+        return [
+            pltpu.make_async_copy(
+                b_ref.at[pl.ds(begin, end - begin)],
+                target.at[pl.ds(begin - offset, end - begin)],
+                sems.at[at + (target is kept) * (slots // chunk)],
+            )
+            for begin, end, target, offset in parts
+        ]
+
+
+    tables = [
+        pltpu.make_async_copy(source, target, table_sems.at[n])
+        for n, (source, target) in enumerate(((cilia_hbm, cilia_ref), (dest_hbm, dest_ref)))
+    ]
+    for copy in tables:
+        copy.start()
     for at in range(slots // chunk):
-        fetch(at).start()
+        for copy in fetches(at):
+            copy.start()
     result[...] = jnp.zeros_like(result)
 
     def clear(i, carry):
@@ -132,11 +173,14 @@
             value = jnp.where(row == 0, high[at:at + 1], jnp.where(row == 1, low[at:at + 1], 0.0))
             lhs[g, :, i * points:(i + 1) * points] = value.astype(BF16)
     lane = lane_iota((1, points))
+    for copy in tables:
+        copy.wait()
     for at in range(slots // chunk):
-        fetch(at).wait()
+        for copy in fetches(at):
+            copy.wait()
         speeds = [
             lax.dot_general(
-                lhs[cilia_ref[0, slot]], held[slot], (((1,), (1,)), ((), ())),
+                lhs[cilia_ref[0, slot]], block(slot), (((1,), (1,)), ((), ())),
                 preferred_element_type=F32,
             )
             for slot in range(at * chunk, (at + 1) * chunk)
@@ -219,18 +263,15 @@
     totals = [jnp.zeros((cil, LANES), F32) for _ in range(comps)]
     for s in range(sources):
         strength = [rows[flat + j * sources + s:flat + j * sources + s + 1] for j in range(comps)]
-        for (i, j), at in PAIRS.items():
-            block = pairs(at, s)
-            totals[i] = totals[i] + block * strength[j]
-            if i != j:
-                totals[j] = totals[j] + block * strength[i]
+        along = [pairs(1 + j, s) for j in range(comps)]
+        projected = sum(along[j] * strength[j] for j in range(comps))
+        direct = pairs(0, s)
+        for i in range(comps):
+            totals[i] = totals[i] + (direct * strength[i] + along[i] * projected)
     far = jnp.concatenate([jnp.sum(t, axis=1, keepdims=True) for t in totals], axis=0)
     dots = rows[flat + comps * sources:flat + comps * sources + 1]
     dots = dots + pltpu.roll(dots, LANES // 2, 1)
     return image + far * profile, dots
-
-
-PAIRS = {(0, 0): 0, (0, 1): 1, (0, 2): 2, (1, 1): 3, (1, 2): 4, (2, 2): 5}
 
 
 def krylov_kernel(comps, cil, sources, total, step, *refs):
@@ -292,10 +333,10 @@
             ]
             inverse = 1.0 / (gap[0] * gap[0] + gap[1] * gap[1] + gap[2] * gap[2] + eps_two)
             amplitude = eps_three * inverse * jnp.sqrt(inverse)
-            slope = amplitude * inverse
-            for (i, j), at in PAIRS.items():
-                block = slope * gap[i] * gap[j]
-                pairs_out[at, s] = block + amplitude if i == j else block
+            slope = jnp.sqrt(amplitude * inverse)
+            pairs_out[0, s] = amplitude
+            for i in range(comps):
+                pairs_out[1 + i, s] = slope * gap[i]
         pairs = lambda at, s: pairs_out[at, s]
     else:
         rows[...] = jnp.dot(sort_ref[...], recv_ref[...], preferred_element_type=F32)
@@ -327,6 +368,14 @@
             entries[GRAM[j, count - 1]] = gram[j, count - 1]
             entries[HESS[j, count - 1]] = heights[j]
         entries[HESS[count, count - 1]] = length
+        if last:
+            units = []
+            for k in range(count - 1):
+                vector = [pick(state, HESS[j, k]) for j in range(k + 2)]
+                weights, unit = orthogonalized(vector, units, k + 2)
+                units.append(unit)
+                entries.update({UPPER[e, k]: weights[e] for e in range(k + 1)})
+                entries.update({UNIT[k, j]: unit[j] for j in range(k + 2)})
     row = pack(entries)
     state_out[...] = row if first else row + state
     for j in range(step):
@@ -377,35 +426,40 @@
     return heights, taken, jnp.sqrt(jnp.maximum(norm, 0.0) + EPSILON)
 
 
+def orthogonalized(vector, units, length):
+    weights = []
+    for e, unit in enumerate(units):
+        used = min(e + 2, length)
+        weight = sum(unit[j] * vector[j] for j in range(used))
+        weights.append(weight)
+        vector = [vector[j] - weight * unit[j] if j < used else vector[j] for j in range(length)]
+    square = sum(entry * entry for entry in vector)
+    size = jnp.sqrt(square)
+    weights.append(size)
+    return weights, [entry / size for entry in vector]
+
+
 def solve_kernel(rows_ref, state_ref, f_ref, v_ref, z_ref, solution_ref, residual_ref):
-    dots = jnp.sum(rows_ref[...], axis=0)
     state = state_ref[...]
+    known = ITERS - 2
+    units = [[pick(state, UNIT[k, j]) for j in range(k + 2)] for k in range(known)]
+    triangle = {(e, k): pick(state, UPPER[e, k]) for k in range(known) for e in range(k + 1)}
+    beta = pick(state, BETA)
+    dots = jnp.sum(rows_ref[...], axis=0, keepdims=True)
     gram, products, square = read_dots(dots, state, ITERS)
     heights, _, length = heights_of(gram, products, square, shifts_of(ITERS), ITERS)
-    zero = jnp.zeros((1, 1), F32)
-    columns = []
-    for k in range(ITERS):
+    for k in range(known, ITERS):
         if k == ITERS - 1:
-            entries = heights + [length]
+            vector = heights + [length]
         else:
-            entries = [pick(state, HESS[j, k]) for j in range(k + 2)]
-        columns.append(entries + [zero] * (ITERS + 1 - len(entries)))
-    units, triangle = [], {}
-    for k in range(ITERS):
-        vector = columns[k]
-        for e in range(k):
-            used = min(e + 2, k + 2)
-            weight = sum(units[e][j] * vector[j] for j in range(used))
-            triangle[e, k] = weight
-            vector = [vector[j] - weight * units[e][j] if j < used else vector[j] for j in range(ITERS + 1)]
-        size = jnp.sqrt(sum(vector[j] * vector[j] for j in range(k + 2)))
-        triangle[k, k] = size
-        units.append([vector[j] / size for j in range(ITERS + 1)])
-    beta = pick(state, BETA)
+            vector = [pick(state, HESS[j, k]) for j in range(k + 2)]
+        weights, unit = orthogonalized(vector, units, k + 2)
+        units.append(unit)
+        triangle.update({(e, k): weights[e] for e in range(k + 1)})
     answers = [None] * ITERS
     for k in reversed(range(ITERS)):
         running = beta * units[k][0]
-        for later in range(k + 1, ITERS):
+        for later in reversed(range(k + 1, ITERS)):
             running = running - triangle[k, later] * answers[later]
         answers[k] = running / triangle[k, k]
     result = answers[0] * v_ref[0]
@@ -437,35 +491,42 @@
     total = cil * rows * cols
     chunk = 4
     struct = lambda *shape, dtype=F32: jax.ShapeDtypeStruct(shape, dtype)
-    vmem, smem = pl.BlockSpec(memory_space=pltpu.VMEM), pl.BlockSpec(memory_space=pltpu.SMEM)
+    vmem, smem, hbm = (pl.BlockSpec(memory_space=m) for m in (pltpu.VMEM, pltpu.SMEM, pltpu.HBM))
     slim = pltpu.CompilerParams(vmem_limit_bytes=4 << 20)
     roomy = pltpu.CompilerParams(vmem_limit_bytes=8 << 20)
     f = forcing.reshape(flat, points)
     stiff = stiffness.reshape(1, cil)
     weights = far_weights.reshape(1, points)
     profile = far_profile.reshape(1, points)
-    cilia = near_cilia.T
-    dest = near_dest.reshape(slots)
-
-    blocks = pltpu.with_memory_space_constraint(near_blocks, pltpu.HBM)
-
-    def exchange(send, x, first):
+    in_hbm = lambda array: pltpu.with_memory_space_constraint(array, pltpu.HBM)
+    blocks = in_hbm(near_blocks)
+    cilia = in_hbm(near_cilia.T)
+    dest = in_hbm(near_dest.reshape(slots))
+
+
+    def exchange(send, x, kept, first):
         arrived = lax.all_to_all(send, "row", split_axis=0, concat_axis=0, tiled=True)
-        near = pl.pallas_call(
+        outs = [struct(cols, TILE, LANES, dtype=BF16)]
+        if first:
+            outs.append(pltpu.VMEM((KEPT, width, width), BF16))
+        near, *fetched = pl.pallas_call(
             functools.partial(near_kernel, comps, cil, chunk, first),
-            out_shape=struct(cols, TILE, LANES, dtype=BF16),
-            in_specs=[smem, smem, smem, vmem, pl.BlockSpec(memory_space=pltpu.HBM)],
-            out_specs=vmem,
+            out_shape=outs,
+            in_specs=[hbm, hbm, smem, vmem, hbm, smem if first else vmem],
+            out_specs=[vmem] * len(outs),
             scratch_shapes=[
                 pltpu.VMEM((cil, TILE, width), BF16),
                 pltpu.VMEM((cols, TILE, points), F32),
                 pltpu.SMEM((cols,), jnp.int32),
-                pltpu.VMEM(blocks.shape, BF16),
-                pltpu.SemaphoreType.DMA((slots // chunk,)),
+                pltpu.VMEM((slots - KEPT, width, width), BF16),
+                pltpu.SMEM(cilia.shape, jnp.int32),
+                pltpu.SMEM(dest.shape, jnp.int32),
+                pltpu.SemaphoreType.DMA((2 * slots // chunk,)),
+                pltpu.SemaphoreType.DMA((2,)),
             ],
             compiler_params=pltpu.CompilerParams(vmem_limit_bytes=16 << 20),
             name="near",
-        )(cilia, dest, near_count, x, blocks)
+        )(cilia, dest, near_count, x, blocks, near_count if first else kept)
         out = pl.pallas_call(
             functools.partial(join_kernel, comps, first),
             out_shape=struct(cols, PITCH[first], LANES, dtype=BF16),
@@ -473,16 +534,22 @@
             name="join",
         )(arrived, near)
         recv = lax.all_to_all(out, "col", split_axis=0, concat_axis=0, tiled=True)
-        return recv.reshape(cols * PITCH[first], LANES)
-
-    send = pl.pallas_call(
+        return recv.reshape(cols * PITCH[first], LANES), fetched[0] if first else kept
+
+    send, x = pl.pallas_call(
         functools.partial(first_kernel, comps, cil),
-        out_shape=struct(rows, TILE, LANES),
+        out_shape=[struct(rows, TILE, LANES), struct(flat, points)],
+        in_specs=[hbm, hbm, hbm],
+        out_specs=[vmem, vmem],
+        scratch_shapes=[
+            pltpu.VMEM((comps, cil), F32),
+            pltpu.VMEM((1, points), F32),
+            pltpu.SemaphoreType.DMA((comps,)),
+        ],
         compiler_params=slim,
         name="first",
-    )(f, positions, weights)
-    recv = exchange(send, f, True)
-    x = f
+    )(in_hbm(f), in_hbm(positions), in_hbm(weights))
+    recv, kept = exchange(send, x, None, True)
     sorted_rows = flat + comps * cols + TILE
     for step in range(1, ITERS + 1):
         first, last = step == 1, step == ITERS
@@ -494,10 +561,10 @@
         if first:
             outs += [
                 struct(sorted_rows, cols * PITCH[False], dtype=BF16),
-                struct(len(PAIRS), cols, cil, LANES),
+                struct(1 + comps, cols, cil, LANES),
             ]
         outs += [
-            struct(rows * cols if last else rows, 1 if last else TILE, LANES),
+            struct(rows * cols, LANES) if last else struct(rows, TILE, LANES),
             struct(flat, points),
             struct(step, flat, points),
             struct(step, flat, points),
@@ -515,7 +582,7 @@
             results = results[2:]
         send, x, vs, zs, state = results
         if not last:
-            recv = exchange(send, x, False)
+            recv, _ = exchange(send, x, kept, False)
     everyone = lax.all_to_all(send, ("row", "col"), split_axis=0, concat_axis=0, tiled=True)
     out, rest = pl.pallas_call(
         solve_kernel, out_shape=[struct(flat, points)] * 2, compiler_params=slim, name="solve"

time: 141 us -> 134 us (0.950)
  local copies, waits for them, and re-layouts: 4.19 us -> 0.02 us
  starting transfers between devices: 24.9 us -> 20.9 us
  waiting for transfers between devices: 4.08 us -> 7.87 us
  Pallas kernels: 31.6 us -> 28.9 us
    unnamed x26 -> x10, local copies, waits for them, and re-layouts: 4.19 us -> 0.02 us
    all_to_all x4, starting transfers between devices: 24.9 us -> 20.9 us  [exchange(): lax.all_to_all(send, 'row', split_axis=0, concat_axis=0, tiled=True)]
    all_to_all x4, waiting for transfers between devices: 4.08 us -> 7.87 us  [exchange(): lax.all_to_all(send, 'row', split_axis=0, concat_axis=0, tiled=True)]
    pallas_call x4, Pallas kernels: 22.3 us -> 19.1 us  [exchange(): pl.pallas_call(functools.partial(near_kernel, comps, cil, chunk, first),...]
  transfers between devices with their start and end apart: 4 -> 4, of which waited for: 3 -> 4; matrix products, arithmetic and copies ran while one was open for 0% -> 0% of each run, Pallas kernels for 16% -> 14%
where the time goes in v2:
time: 134 us; the launch traced here: 133 us
  blocking collectives  74.2 us (55%)
  Pallas kernels  28.9 us (22%)
  starting transfers between devices  20.9 us (16%)
  waiting for transfers between devices  7.87 us (6%)
  between operations  1.39 us (1%)
    all_to_all x4, blocking collectives, exchange(): recv = lax.all_to_all(out, 'col', split_axis=0, concat_axis=0, tiled=True)  55.2 us
    all_to_all x4, starting transfers between devices, exchange(): lax.all_to_all(send, 'row', split_axis=0, concat_axis=0, tiled=True)  20.9 us
    pallas_call x4, Pallas kernels, exchange(): pl.pallas_call(functools.partial(near_kernel, comps, cil, chunk, first),...  19.1 us
    all_to_all x1, blocking collectives, on_device(): lax.all_to_all(send, ('row', 'col'), split_axis=0, concat_axis=0, tiled=T...  19 us
    all_to_all x4, waiting for transfers between devices, exchange(): lax.all_to_all(send, 'row', split_axis=0, concat_axis=0, tiled=True)  7.87 us
    pallas_call x4, Pallas kernels, on_device(): pl.pallas_call(functools.partial(krylov_kernel, comps, cil, cols, total,...  5.87 us
  transfers between devices with their start and end apart: 4, of which 4 were waited for; matrix products, arithmetic and copies ran while one was open for 0% of the time, Pallas kernels for 14%

profile of v2, /device:TPU:1, one launch (start us, length us, event | category | flops | bytes accessed | tf_op | source)
XLA Modules:
  0.0 133.3 jit_solution(4583072815178450434)
XLA Ops:
  0.6 0.0 copy-start.4
  0.6 0.0 copy-start.3
  0.7 0.0 copy-start.2
  0.7 0.0 copy-start.1
  0.7 1.5 %first.1 = (f32[8,8,128]{2,1,0:T(8,128)}, f32[48,128]{1,0:T(8,128)S(1)}) custom-call(f32[48,128]{1,0:T(8,128)} %bitcast.22, f32[3,16]{1,0:T(4,128)} %refs_5_.1, f32[1,128]{1,0:T(1,128)} %bitcast.32), custom_call_target="tpu_custom_call" | custom-call | tf_op jit(solution)/shard_map/first/pallas_call | solution.py:539
  2.2 9.0 %all-to-all-start = ((f32[8,8,128]{2,1,0:T(8,128)}), f32[8,8,128]{2,1,0:T(8,128)S(1)}, u32[]{:S(2)}, u32[]{:S(2)}) async-start(f32[8,8,128]{2,1,0:T(8,128)} %get-tuple-element.29), calls=%async_computation | async-start | bytes 65536 | tf_op jit(solution)/shard_map/all_to_all | solution.py:508
  11.9 5.1 %near.4 = (bf16[32,8,128]{2,1,0:T(8,128)(2,1)S(1)}, bf16[6,384,384]{2,1,0:T(8,128)(2,1)S(1)}) custom-call(s32[2,32]{1,0:T(2,128)} %bitcast.36, s32[32]{0:T(128)} %bitcast.40, s32[1]{0:T(128)S(6)} %copy.12.count_ref.kept_in, f32[48,128]{1,0:T(8,128)S(1)} %get-tuple-element.30.x_ref.refs_1_, bf16[32,384,384]{2,1,0:T(8,128)(2,1)} %b_ref.7, ...), custom_call_target="tpu_custom_call" | custom-call | tf_op jit(solution)/shard_map/near/pallas_call | solution.py:512
  17.0 1.1 all-to-all-done.rows_ref
  18.1 0.1 join.4
  18.2 17.3 %all_to_all.51 = bf16[32,24,128]{2,1,0:T(8,128)(2,1)S(1)} all-to-all(bf16[32,24,128]{2,1,0:T(8,128)(2,1)S(1)} %join.4), channel_id=1, replica_groups=mesh['row'=8,'col'=32] {'col'}, dimensions={0} | all-to-all | bytes 393216 | tf_op jit(solution)/shard_map/all_to_all | solution.py:536
  35.5 0.0 copy-done.4
  35.5 0.0 copy-done.3
  35.5 0.0 copy-done.2
  35.5 0.0 copy-done.1
  35.5 2.0 %krylov.4 = (bf16[152,512]{1,0:T(8,128)(2,1)S(1)}, f32[4,32,16,128]{3,2,1,0:T(8,128)S(1)}, f32[8,8,128]{2,1,0:T(8,128)}, f32[48,128]{1,0:T(8,128)S(1)}, f32[1,48...) custom-call(bf16[768,128]{1,0:T(8,128)(2,1)S(1)} %bitcast.16, ...), custom_call_target="tpu_custom_call" | custom-call | tf_op jit(solution)/shard_map/krylov/pallas_call | solution.py:573
  37.5 4.7 %all-to-all-start.2 = ((f32[8,8,128]{2,1,0:T(8,128)}), f32[8,8,128]{2,1,0:T(8,128)S(1)}, u32[]{:S(2)}, u32[]{:S(2)}) async-start(f32[8,8,128]{2,1,0:T(8,128)} %get-tuple-element.32), calls=%async_computation.2 | async-start | bytes 65536 | tf_op jit(solution)/shard_map/all_to_all | solution.py:508
  42.2 4.7 %near.5.near_ref = bf16[32,8,128]{2,1,0:T(8,128)(2,1)S(1)} custom-call(s32[2,32]{1,0:T(2,128)} %bitcast.37, s32[32]{0:T(128)} %bitcast.41, s32[1]{0:T(128)S(6)} %copy.12.count_ref.kept_in, f32[48,128]{1,0:T(8,128)S(1)} %get-tuple-element.33.x_ref.refs_1_, bf16[32,384,384]{2,1,0:T(8,128)(2,1)} %b_ref.7, bf16[6,384,384]{2,1,0:T(8,128)(2,1)S(1)} %get-tuple-element.34.kept_in), custom_call_target="tpu_custom_call" | custom-call | tf_op jit(solution)/shard_map/near/pallas_call | solution.py:512
  46.9 2.2 %all-to-all-done.2.rows_ref = f32[8,8,128]{2,1,0:T(8,128)S(1)} async-done(((f32[8,8,128]{2,1,0:T(8,128)}), f32[8,8,128]{2,1,0:T(8,128)S(1)}, u32[]{:S(2)}, u32[]{:S(2)}) %all-to-all-start.2) | async-done | bytes 32800 | tf_op jit(solution)/shard_map/all_to_all | solution.py:508
  49.1 0.1 join.5
  49.2 12.7 %all_to_all.52 = bf16[32,16,128]{2,1,0:T(8,128)(2,1)S(1)} all-to-all(bf16[32,16,128]{2,1,0:T(8,128)(2,1)S(1)} %join.5), channel_id=1, replica_groups=mesh['row'=8,'col'=32] {'col'}, dimensions={0} | all-to-all | bytes 262144 | tf_op jit(solution)/shard_map/all_to_all | solution.py:536
  61.9 1.3 krylov.5
  63.1 3.6 %all-to-all-start.4 = ((f32[8,8,128]{2,1,0:T(8,128)}), f32[8,8,128]{2,1,0:T(8,128)S(1)}, u32[]{:S(2)}, u32[]{:S(2)}) async-start(f32[8,8,128]{2,1,0:T(8,128)} %get-tuple-element.40), calls=%async_computation.4 | async-start | bytes 65536 | tf_op jit(solution)/shard_map/all_to_all | solution.py:508
  66.7 4.7 %near.6.near_ref = bf16[32,8,128]{2,1,0:T(8,128)(2,1)S(1)} custom-call(s32[2,32]{1,0:T(2,128)} %bitcast.38, s32[32]{0:T(128)} %bitcast.42, s32[1]{0:T(128)S(6)} %copy.12.count_ref.kept_in, f32[48,128]{1,0:T(8,128)S(1)} %get-tuple-element.41.x_ref.refs_1_, bf16[32,384,384]{2,1,0:T(8,128)(2,1)} %b_ref.7, bf16[6,384,384]{2,1,0:T(8,128)(2,1)S(1)} %get-tuple-element.34.kept_in), custom_call_target="tpu_custom_call" | custom-call | tf_op jit(solution)/shard_map/near/pallas_call | solution.py:512
  71.4 0.0 copy-start
  71.4 2.3 %all-to-all-done.4.rows_ref = f32[8,8,128]{2,1,0:T(8,128)S(1)} async-done(((f32[8,8,128]{2,1,0:T(8,128)}), f32[8,8,128]{2,1,0:T(8,128)S(1)}, u32[]{:S(2)}, u32[]{:S(2)}) %all-to-all-start.4) | async-done | bytes 32800 | tf_op jit(solution)/shard_map/all_to_all | solution.py:508
  73.7 0.1 join.6
  73.8 12.6 %all_to_all.53 = bf16[32,16,128]{2,1,0:T(8,128)(2,1)S(1)} all-to-all(bf16[32,16,128]{2,1,0:T(8,128)(2,1)S(1)} %join.6), channel_id=1, replica_groups=mesh['row'=8,'col'=32] {'col'}, dimensions={0} | all-to-all | bytes 262144 | tf_op jit(solution)/shard_map/all_to_all | solution.py:536
  86.4 1.4 %krylov.6 = (f32[8,8,128]{2,1,0:T(8,128)}, f32[48,128]{1,0:T(8,128)S(1)}, f32[3,48,128]{2,1,0:T(8,128)S(1)}, f32[3,48,128]{2,1,0:T(8,128)S(1)}, f32[1,128]{1,0:T(1,128)S(1)}) custom-call(bf16[512,128]{1,0:T(8,128)(2,1)S(1)} %bitcast.18, f32[48,128]{1,0:T(8,128)S(1)} %get-tuple-element.41.x_ref.refs_1_, f32[1,16]{1,0:T(1,128)S(1)} %bitcast.26, ...), custom_call_target="tpu_custom_call" | custom-call | tf_op jit(solution)/shard_map/krylov/pallas_call | solution.py:573
  87.8 3.6 %all-to-all-start.6 = ((f32[8,8,128]{2,1,0:T(8,128)}), f32[8,8,128]{2,1,0:T(8,128)S(1)}, u32[]{:S(2)}, u32[]{:S(2)}) async-start(f32[8,8,128]{2,1,0:T(8,128)} %get-tuple-element.45), calls=%async_computation.6 | async-start | bytes 65536 | tf_op jit(solution)/shard_map/all_to_all | solution.py:508
  91.4 4.7 %near.7.near_ref = bf16[32,8,128]{2,1,0:T(8,128)(2,1)S(1)} custom-call(s32[2,32]{1,0:T(2,128)} %bitcast.39, s32[32]{0:T(128)} %bitcast.43, s32[1]{0:T(128)S(6)} %copy.12.count_ref.kept_in, f32[48,128]{1,0:T(8,128)S(1)} %get-tuple-element.46.x_ref.refs_1_, bf16[32,384,384]{2,1,0:T(8,128)(2,1)} %b_ref.7, bf16[6,384,384]{2,1,0:T(8,128)(2,1)S(1)} %get-tuple-element.34.kept_in), custom_call_target="tpu_custom_call" | custom-call | tf_op jit(solution)/shard_map/near/pallas_call | solution.py:512
  96.0 2.3 %all-to-all-done.6.rows_ref = f32[8,8,128]{2,1,0:T(8,128)S(1)} async-done(((f32[8,8,128]{2,1,0:T(8,128)}), f32[8,8,128]{2,1,0:T(8,128)S(1)}, u32[]{:S(2)}, u32[]{:S(2)}) %all-to-all-start.6) | async-done | bytes 32800 | tf_op jit(solution)/shard_map/all_to_all | solution.py:508
  98.3 0.1 join.7
  98.4 12.6 %all_to_all.54 = bf16[32,16,128]{2,1,0:T(8,128)(2,1)S(1)} all-to-all(bf16[32,16,128]{2,1,0:T(8,128)(2,1)S(1)} %join.7), channel_id=1, replica_groups=mesh['row'=8,'col'=32] {'col'}, dimensions={0} | all-to-all | bytes 262144 | tf_op jit(solution)/shard_map/all_to_all | solution.py:536
  111.0 1.2 krylov.7
  112.3 19.0 %all_to_all.55 = f32[256,1,128]{2,1,0:T(1,128)S(1)} all-to-all(f32[256,1,128]{2,1,0:T(1,128)S(1)} %bitcast.21), channel_id=1, replica_groups=mesh['row'=8,'col'=32] {'row','col'}, dimensions={0} | all-to-all | bytes 262144 | tf_op jit(solution)/shard_map/all_to_all | solution.py:586
  131.3 0.0 copy-done
  131.3 2.0 %solve.1 = (f32[48,128]{1,0:T(8,128)}, f32[48,128]{1,0:T(8,128)}) custom-call(f32[256,128]{1,0:T(8,128)S(1)} %bitcast.19, f32[1,128]{1,0:T(1,128)S(1)} %get-tuple-element.51.state_ref, f32[48,128]{1,0:T(8,128)S(1)} %bitcast.23, f32[4,48,128]{2,1,0:T(8,128)S(1)} %get-tuple-element.52.v_ref, f32[4,48,128]{2,1,0:T(8,128)S(1)} %get-tuple-element.53.z_ref), custom_call_target="tpu_custom_call" | custom-call | tf_op jit(solution)/shard_map/solve/pallas_call | solution.py:587
Async XLA Ops:
  0.6 34.9 %copy-start.4 = (f32[3,16]{1,0:T(4,128)S(1)}, f32[3,16]{1,0:T(4,128)}, u32[]{:S(2)}) copy-start(f32[3,16]{1,0:T(4,128)} %refs_5_.1) | copy-start | bytes 580
  0.6 34.9 %copy-start.3 = (f32[128]{0:T(128)S(1)}, f32[128]{0:T(128)}, u32[]{:S(2)}) copy-start(f32[128]{0:T(128)} %param.12) | copy-start | bytes 1540
  0.7 34.9 %copy-start.2 = (f32[128]{0:T(128)S(1)}, f32[128]{0:T(128)}, u32[]{:S(2)}) copy-start(f32[128]{0:T(128)} %param.13) | copy-start | bytes 1540
  0.7 34.9 %copy-start.1 = (f32[16]{0:T(128)S(1)}, f32[16]{0:T(128)}, u32[]{:S(2)}) copy-start(f32[16]{0:T(128)} %param.10) | copy-start | bytes 196
  2.2 15.9 %all-to-all-start = ((f32[8,8,128]{2,1,0:T(8,128)}), f32[8,8,128]{2,1,0:T(8,128)S(1)}, u32[]{:S(2)}, u32[]{:S(2)}) async-start(f32[8,8,128]{2,1,0:T(8,128)} %get-tuple-element.29), calls=%async_computation | async-start | bytes 65536 | tf_op jit(solution)/shard_map/all_to_all | solution.py:508
  37.5 11.6 %all-to-all-start.2 = ((f32[8,8,128]{2,1,0:T(8,128)}), f32[8,8,128]{2,1,0:T(8,128)S(1)}, u32[]{:S(2)}, u32[]{:S(2)}) async-start(f32[8,8,128]{2,1,0:T(8,128)} %get-tuple-element.32), calls=%async_computation.2 | async-start | bytes 65536 | tf_op jit(solution)/shard_map/all_to_all | solution.py:508
  63.1 10.6 %all-to-all-start.4 = ((f32[8,8,128]{2,1,0:T(8,128)}), f32[8,8,128]{2,1,0:T(8,128)S(1)}, u32[]{:S(2)}, u32[]{:S(2)}) async-start(f32[8,8,128]{2,1,0:T(8,128)} %get-tuple-element.40), calls=%async_computation.4 | async-start | bytes 65536 | tf_op jit(solution)/shard_map/all_to_all | solution.py:508
  71.4 59.9 %copy-start = (f32[3,16,128]{2,1,0:T(8,128)S(1)}, f32[3,16,128]{2,1,0:T(8,128)}, u32[]{:S(2)}) copy-start(f32[3,16,128]{2,1,0:T(8,128)} %param.9) | copy-start | bytes 73732
  87.8 10.6 %all-to-all-start.6 = ((f32[8,8,128]{2,1,0:T(8,128)}), f32[8,8,128]{2,1,0:T(8,128)S(1)}, u32[]{:S(2)}, u32[]{:S(2)}) async-start(f32[8,8,128]{2,1,0:T(8,128)} %get-tuple-element.45), calls=%async_computation.6 | async-start | bytes 65536 | tf_op jit(solution)/shard_map/all_to_all | solution.py:508

commit v3 on v2

--- a/solution.py
+++ b/solution.py
@@ -113,25 +113,30 @@
 
 TILE = 8
 KEPT = 6
+CHUNKS = (8, 8, 8, 8)
 META = 6
 DOTS = 14
 PITCH = {True: 24, False: 16}
 
 
-def near_kernel(comps, cil, chunk, first, cilia_hbm, dest_hbm, count_ref, x_ref, b_ref, kept_in, *refs):
+def near_kernel(comps, cil, first, cilia_hbm, table_hbm, count_ref, x_ref, b_ref, *refs):
+    refs = list(refs)
+    if not first:
+        kept = refs.pop(0)
+    out_ref = refs.pop(0)
     if first:
-        out_ref, kept, lhs, result, used, held, cilia_ref, dest_ref, sems, table_sems = refs
-    else:
-        out_ref, lhs, result, used, held, cilia_ref, dest_ref, sems, table_sems = refs
-        kept = kept_in
+        kept, place_ref = refs[:2]
+        refs = refs[2:]
+    lhs, result, used, held, cilia_ref, table_ref, sems, table_sems = refs
     points = x_ref.shape[1]
     slots = b_ref.shape[0]
+    bounds = [(sum(CHUNKS[:n]), sum(CHUNKS[:n + 1])) for n in range(len(CHUNKS))]
 
     def block(slot):
         return kept[slot] if slot < KEPT else held[slot - KEPT]
 
-    def fetches(at):
-        start, stop = at * chunk, (at + 1) * chunk
+    def fetches(n):
+        start, stop = bounds[n]
         parts = []
         if first and start < KEPT:
             parts.append((start, min(stop, KEPT), kept, 0))
@@ -141,28 +146,21 @@
             pltpu.make_async_copy(
                 b_ref.at[pl.ds(begin, end - begin)],
                 target.at[pl.ds(begin - offset, end - begin)],
-                sems.at[at + (target is kept) * (slots // chunk)],
+                sems.at[n + (target is kept) * len(CHUNKS)],
             )
             for begin, end, target, offset in parts
         ]
 
-
     tables = [
         pltpu.make_async_copy(source, target, table_sems.at[n])
-        for n, (source, target) in enumerate(((cilia_hbm, cilia_ref), (dest_hbm, dest_ref)))
+        for n, (source, target) in enumerate(((cilia_hbm, cilia_ref), (table_hbm, table_ref)))
     ]
     for copy in tables:
         copy.start()
-    for at in range(slots // chunk):
-        for copy in fetches(at):
+    for n in range(len(CHUNKS)):
+        for copy in fetches(n):
             copy.start()
     result[...] = jnp.zeros_like(result)
-
-    def clear(i, carry):
-        used[i] = 0
-        return carry
-
-    lax.fori_loop(0, used.shape[0], clear, 0)
     x = x_ref[...]
     high = x.astype(BF16).astype(F32)
     low = x - high
@@ -172,33 +170,37 @@
             at = i * cil + g
             value = jnp.where(row == 0, high[at:at + 1], jnp.where(row == 1, low[at:at + 1], 0.0))
             lhs[g, :, i * points:(i + 1) * points] = value.astype(BF16)
-    lane = lane_iota((1, points))
     for copy in tables:
         copy.wait()
-    for at in range(slots // chunk):
-        for copy in fetches(at):
+    if first:
+        lane = lane_iota((1, points))
+        for dest in range(used.shape[0]):
+            used[dest] = 0
+        for slot in range(slots):
+            dest = table_ref[slot]
+            rank = used[dest]
+            used[dest] = rank + 1
+            place_ref[slot] = dest * TILE + rank * comps
+            at = pl.ds(dest * TILE + META, 1)
+            target = cilia_ref[1, slot].astype(F32)
+            result[at, :] = jnp.where(lane == rank, target, result[at, :])
+    else:
+        place_ref = table_ref
+    for n, (start, stop) in enumerate(bounds):
+        for copy in fetches(n):
             copy.wait()
         speeds = [
             lax.dot_general(
                 lhs[cilia_ref[0, slot]], block(slot), (((1,), (1,)), ((), ())),
                 preferred_element_type=F32,
             )
-            for slot in range(at * chunk, (at + 1) * chunk)
+            for slot in range(start, stop)
         ]
-        for s in range(chunk):
-            slot = at * chunk + s
-            dest = dest_ref[slot]
-            rank = used[dest]
-            used[dest] = rank + 1
-            live = slot < count_ref[0]
-            speed = jnp.where(live, speeds[s][0:1] + speeds[s][1:2], 0.0)
+        for slot, speed in zip(range(start, stop), speeds):
+            speed = jnp.where(slot < count_ref[0], speed[0:1] + speed[1:2], 0.0)
             for i in range(comps):
-                result[dest, pl.ds(rank * comps + i, 1), :] = speed[:, i * points:(i + 1) * points]
-            if first:
-                target = cilia_ref[1, slot].astype(F32)
-                before = result[dest, META:META + 1, :]
-                result[dest, META:META + 1, :] = jnp.where(lane == rank, target, before)
-    out_ref[...] = result[...].astype(BF16)
+                result[pl.ds(place_ref[slot] + i, 1), :] = speed[:, i * points:(i + 1) * points]
+    out_ref[...] = result[...].astype(BF16).reshape(out_ref.shape)
 
 
 def join_kernel(comps, first, rows_ref, near_ref, send_ref):
@@ -489,7 +491,6 @@
     width = comps * points
     flat = comps * cil
     total = cil * rows * cols
-    chunk = 4
     struct = lambda *shape, dtype=F32: jax.ShapeDtypeStruct(shape, dtype)
     vmem, smem, hbm = (pl.BlockSpec(memory_space=m) for m in (pltpu.VMEM, pltpu.SMEM, pltpu.HBM))
     slim = pltpu.CompilerParams(vmem_limit_bytes=4 << 20)
@@ -506,27 +507,31 @@
 
     def exchange(send, x, kept, first):
         arrived = lax.all_to_all(send, "row", split_axis=0, concat_axis=0, tiled=True)
-        outs = [struct(cols, TILE, LANES, dtype=BF16)]
+        outs, specs = [struct(cols, TILE, LANES, dtype=BF16)], [vmem]
         if first:
-            outs.append(pltpu.VMEM((KEPT, width, width), BF16))
+            table, extra = dest, ()
+            outs += [pltpu.VMEM((KEPT, width, width), BF16), struct(slots, dtype=jnp.int32)]
+            specs += [vmem, smem]
+        else:
+            table, extra = in_hbm(kept[1]), kept[:1]
         near, *fetched = pl.pallas_call(
-            functools.partial(near_kernel, comps, cil, chunk, first),
+            functools.partial(near_kernel, comps, cil, first),
             out_shape=outs,
-            in_specs=[hbm, hbm, smem, vmem, hbm, smem if first else vmem],
-            out_specs=[vmem] * len(outs),
+            in_specs=[hbm, hbm, smem, vmem, hbm] + [vmem] * len(extra),
+            out_specs=specs,
             scratch_shapes=[
                 pltpu.VMEM((cil, TILE, width), BF16),
-                pltpu.VMEM((cols, TILE, points), F32),
+                pltpu.VMEM((cols * TILE, points), F32),
                 pltpu.SMEM((cols,), jnp.int32),
                 pltpu.VMEM((slots - KEPT, width, width), BF16),
                 pltpu.SMEM(cilia.shape, jnp.int32),
                 pltpu.SMEM(dest.shape, jnp.int32),
-                pltpu.SemaphoreType.DMA((2 * slots // chunk,)),
+                pltpu.SemaphoreType.DMA((2 * len(CHUNKS),)),
                 pltpu.SemaphoreType.DMA((2,)),
             ],
             compiler_params=pltpu.CompilerParams(vmem_limit_bytes=16 << 20),
             name="near",
-        )(cilia, dest, near_count, x, blocks, near_count if first else kept)
+        )(cilia, table, near_count, x, blocks, *extra)
         out = pl.pallas_call(
             functools.partial(join_kernel, comps, first),
             out_shape=struct(cols, PITCH[first], LANES, dtype=BF16),
@@ -534,7 +539,7 @@
             name="join",
         )(arrived, near)
         recv = lax.all_to_all(out, "col", split_axis=0, concat_axis=0, tiled=True)
-        return recv.reshape(cols * PITCH[first], LANES), fetched[0] if first else kept
+        return recv.reshape(cols * PITCH[first], LANES), fetched if first else kept
 
     send, x = pl.pallas_call(
         functools.partial(first_kernel, comps, cil),

time: 134 us -> 133 us (level)
  no operation moved by 1% of the time
where the time goes in v3:
time: 133 us; the launch traced here: 132 us
  blocking collectives  73.9 us (56%)
  Pallas kernels  27.7 us (21%)
  starting transfers between devices  20.2 us (15%)
  waiting for transfers between devices  8.9 us (7%)
  between operations  1.42 us (1%)
    all_to_all x4, blocking collectives, exchange(): recv = lax.all_to_all(out, 'col', split_axis=0, concat_axis=0, tiled=True)  55.2 us
    all_to_all x4, starting transfers between devices, exchange(): lax.all_to_all(send, 'row', split_axis=0, concat_axis=0, tiled=True)  20.2 us
    all_to_all x1, blocking collectives, on_device(): lax.all_to_all(send, ('row', 'col'), split_axis=0, concat_axis=0, tiled=T...  18.7 us
    pallas_call x4, Pallas kernels, exchange(): pl.pallas_call(functools.partial(near_kernel, comps, cil, first), out_sha...  18 us
    all_to_all x4, waiting for transfers between devices, exchange(): lax.all_to_all(send, 'row', split_axis=0, concat_axis=0, tiled=True)  8.9 us
    pallas_call x4, Pallas kernels, on_device(): pl.pallas_call(functools.partial(krylov_kernel, comps, cil, cols, total,...  5.86 us
  transfers between devices with their start and end apart: 4, of which 4 were waited for; matrix products, arithmetic and copies ran while one was open for 0% of the time, Pallas kernels for 14%

profile of v3, /device:TPU:1, one launch (start us, length us, event | category | flops | bytes accessed | tf_op | source)
XLA Modules:
  0.0 132.1 jit_solution(15086925342068076167)
XLA Ops:
  0.6 0.0 copy-start.4
  0.6 0.0 copy-start.3
  0.7 0.0 copy-start.2
  0.7 0.0 copy-start.1
  0.7 1.5 %first.1 = (f32[8,8,128]{2,1,0:T(8,128)}, f32[48,128]{1,0:T(8,128)S(1)}) custom-call(f32[48,128]{1,0:T(8,128)} %bitcast.22, f32[3,16]{1,0:T(4,128)} %refs_5_.1, f32[1,128]{1,0:T(1,128)} %bitcast.32), custom_call_target="tpu_custom_call" | custom-call | tf_op jit(solution)/shard_map/first/pallas_call | solution.py:544
  2.2 9.0 %all-to-all-start = ((f32[8,8,128]{2,1,0:T(8,128)}), f32[8,8,128]{2,1,0:T(8,128)S(1)}, u32[]{:S(2)}, u32[]{:S(2)}) async-start(f32[8,8,128]{2,1,0:T(8,128)} %get-tuple-element.30), calls=%async_computation | async-start | bytes 65536 | tf_op jit(solution)/shard_map/all_to_all | solution.py:509
  11.9 4.9 %near.4 = (bf16[32,8,128]{2,1,0:T(8,128)(2,1)S(1)}, bf16[6,384,384]{2,1,0:T(8,128)(2,1)S(1)}, s32[32]{0:T(128)S(1)}) custom-call(s32[2,32]{1,0:T(2,128)} %bitcast.36, s32[32]{0:T(128)} %bitcast.40, s32[1]{0:T(128)S(6)} %copy.12.count_ref, f32[48,128]{1,0:T(8,128)S(1)} %get-tuple-element.31.x_ref.refs_1_, bf16[32,384,384]{2,1,0:T(8,128)(2,1)} %b_ref.7), custom_call_target="tpu_custom_call" | custom-call | tf_op jit(solution)/shard_map/near/pallas_call | solution.py:517
  16.8 0.0 copy-start.5
  16.8 1.3 all-to-all-done.rows_ref
  18.1 0.1 join.4
  18.2 17.3 %all_to_all.51 = bf16[32,24,128]{2,1,0:T(8,128)(2,1)S(1)} all-to-all(bf16[32,24,128]{2,1,0:T(8,128)(2,1)S(1)} %join.4), channel_id=1, replica_groups=mesh['row'=8,'col'=32] {'col'}, dimensions={0} | all-to-all | bytes 393216 | tf_op jit(solution)/shard_map/all_to_all | solution.py:541
  35.5 0.0 copy-done.4
  35.5 0.0 copy-done.3
  35.5 0.0 copy-done.2
  35.5 0.0 copy-done.1
  35.5 2.0 %krylov.4 = (bf16[152,512]{1,0:T(8,128)(2,1)S(1)}, f32[4,32,16,128]{3,2,1,0:T(8,128)S(1)}, f32[8,8,128]{2,1,0:T(8,128)}, f32[48,128]{1,0:T(8,128)S(1)}, f32[1,48...) custom-call(bf16[768,128]{1,0:T(8,128)(2,1)S(1)} %bitcast.16, ...), custom_call_target="tpu_custom_call" | custom-call | tf_op jit(solution)/shard_map/krylov/pallas_call | solution.py:578
  37.5 4.5 %all-to-all-start.2 = ((f32[8,8,128]{2,1,0:T(8,128)}), f32[8,8,128]{2,1,0:T(8,128)S(1)}, u32[]{:S(2)}, u32[]{:S(2)}) async-start(f32[8,8,128]{2,1,0:T(8,128)} %get-tuple-element.33), calls=%async_computation.2 | async-start | bytes 65536 | tf_op jit(solution)/shard_map/all_to_all | solution.py:509
  42.0 0.0 copy-done.5
  42.0 4.4 %near.5.near_ref = bf16[32,8,128]{2,1,0:T(8,128)(2,1)S(1)} custom-call(s32[2,32]{1,0:T(2,128)} %bitcast.37, s32[32]{0:T(128)} %copy-done.5, s32[1]{0:T(128)S(6)} %copy.12.count_ref, f32[48,128]{1,0:T(8,128)S(1)} %get-tuple-element.35.x_ref.refs_1_, bf16[32,384,384]{2,1,0:T(8,128)(2,1)} %b_ref.7, bf16[6,384,384]{2,1,0:T(8,128)(2,1)S(1)} %get-tuple-element.36.refs_0_), custom_call_target="tpu_custom_call" | custom-call | tf_op jit(solution)/shard_map/near/pallas_call | solution.py:517
  46.4 2.5 %all-to-all-done.2.rows_ref = f32[8,8,128]{2,1,0:T(8,128)S(1)} async-done(((f32[8,8,128]{2,1,0:T(8,128)}), f32[8,8,128]{2,1,0:T(8,128)S(1)}, u32[]{:S(2)}, u32[]{:S(2)}) %all-to-all-start.2) | async-done | bytes 32800 | tf_op jit(solution)/shard_map/all_to_all | solution.py:509
  48.9 0.1 join.5
  49.0 12.7 %all_to_all.52 = bf16[32,16,128]{2,1,0:T(8,128)(2,1)S(1)} all-to-all(bf16[32,16,128]{2,1,0:T(8,128)(2,1)S(1)} %join.5), channel_id=1, replica_groups=mesh['row'=8,'col'=32] {'col'}, dimensions={0} | all-to-all | bytes 262144 | tf_op jit(solution)/shard_map/all_to_all | solution.py:541
  61.6 1.3 krylov.5
  62.9 3.3 %all-to-all-start.4 = ((f32[8,8,128]{2,1,0:T(8,128)}), f32[8,8,128]{2,1,0:T(8,128)S(1)}, u32[]{:S(2)}, u32[]{:S(2)}) async-start(f32[8,8,128]{2,1,0:T(8,128)} %get-tuple-element.42), calls=%async_computation.4 | async-start | bytes 65536 | tf_op jit(solution)/shard_map/all_to_all | solution.py:509
  66.3 4.4 %near.6.near_ref = bf16[32,8,128]{2,1,0:T(8,128)(2,1)S(1)} custom-call(s32[2,32]{1,0:T(2,128)} %bitcast.38, s32[32]{0:T(128)} %copy-done.5, s32[1]{0:T(128)S(6)} %copy.12.count_ref, f32[48,128]{1,0:T(8,128)S(1)} %get-tuple-element.43.x_ref.refs_1_, bf16[32,384,384]{2,1,0:T(8,128)(2,1)} %b_ref.7, bf16[6,384,384]{2,1,0:T(8,128)(2,1)S(1)} %get-tuple-element.36.refs_0_), custom_call_target="tpu_custom_call" | custom-call | tf_op jit(solution)/shard_map/near/pallas_call | solution.py:517
  70.6 0.0 copy-start
  70.6 2.5 %all-to-all-done.4.rows_ref = f32[8,8,128]{2,1,0:T(8,128)S(1)} async-done(((f32[8,8,128]{2,1,0:T(8,128)}), f32[8,8,128]{2,1,0:T(8,128)S(1)}, u32[]{:S(2)}, u32[]{:S(2)}) %all-to-all-start.4) | async-done | bytes 32800 | tf_op jit(solution)/shard_map/all_to_all | solution.py:509
  73.2 0.1 join.6
  73.3 12.6 %all_to_all.53 = bf16[32,16,128]{2,1,0:T(8,128)(2,1)S(1)} all-to-all(bf16[32,16,128]{2,1,0:T(8,128)(2,1)S(1)} %join.6), channel_id=1, replica_groups=mesh['row'=8,'col'=32] {'col'}, dimensions={0} | all-to-all | bytes 262144 | tf_op jit(solution)/shard_map/all_to_all | solution.py:541
  85.9 1.4 %krylov.6 = (f32[8,8,128]{2,1,0:T(8,128)}, f32[48,128]{1,0:T(8,128)S(1)}, f32[3,48,128]{2,1,0:T(8,128)S(1)}, f32[3,48,128]{2,1,0:T(8,128)S(1)}, f32[1,128]{1,0:T(1,128)S(1)}) custom-call(bf16[512,128]{1,0:T(8,128)(2,1)S(1)} %bitcast.18, f32[48,128]{1,0:T(8,128)S(1)} %get-tuple-element.43.x_ref.refs_1_, f32[1,16]{1,0:T(1,128)S(1)} %bitcast.26, ...), custom_call_target="tpu_custom_call" | custom-call | tf_op jit(solution)/shard_map/krylov/pallas_call | solution.py:578
  87.2 3.3 %all-to-all-start.6 = ((f32[8,8,128]{2,1,0:T(8,128)}), f32[8,8,128]{2,1,0:T(8,128)S(1)}, u32[]{:S(2)}, u32[]{:S(2)}) async-start(f32[8,8,128]{2,1,0:T(8,128)} %get-tuple-element.47), calls=%async_computation.6 | async-start | bytes 65536 | tf_op jit(solution)/shard_map/all_to_all | solution.py:509
  90.6 4.4 %near.7.near_ref = bf16[32,8,128]{2,1,0:T(8,128)(2,1)S(1)} custom-call(s32[2,32]{1,0:T(2,128)} %bitcast.39, s32[32]{0:T(128)} %copy-done.5, s32[1]{0:T(128)S(6)} %copy.12.count_ref, f32[48,128]{1,0:T(8,128)S(1)} %get-tuple-element.48.x_ref.refs_1_, bf16[32,384,384]{2,1,0:T(8,128)(2,1)} %b_ref.7, bf16[6,384,384]{2,1,0:T(8,128)(2,1)S(1)} %get-tuple-element.36.refs_0_), custom_call_target="tpu_custom_call" | custom-call | tf_op jit(solution)/shard_map/near/pallas_call | solution.py:517
  94.9 2.6 %all-to-all-done.6.rows_ref = f32[8,8,128]{2,1,0:T(8,128)S(1)} async-done(((f32[8,8,128]{2,1,0:T(8,128)}), f32[8,8,128]{2,1,0:T(8,128)S(1)}, u32[]{:S(2)}, u32[]{:S(2)}) %all-to-all-start.6) | async-done | bytes 32800 | tf_op jit(solution)/shard_map/all_to_all | solution.py:509
  97.5 0.1 join.7
  97.6 12.6 %all_to_all.54 = bf16[32,16,128]{2,1,0:T(8,128)(2,1)S(1)} all-to-all(bf16[32,16,128]{2,1,0:T(8,128)(2,1)S(1)} %join.7), channel_id=1, replica_groups=mesh['row'=8,'col'=32] {'col'}, dimensions={0} | all-to-all | bytes 262144 | tf_op jit(solution)/shard_map/all_to_all | solution.py:541
  110.2 1.2 krylov.7
  111.4 18.7 %all_to_all.55 = f32[256,1,128]{2,1,0:T(1,128)S(1)} all-to-all(f32[256,1,128]{2,1,0:T(1,128)S(1)} %bitcast.21), channel_id=1, replica_groups=mesh['row'=8,'col'=32] {'row','col'}, dimensions={0} | all-to-all | bytes 262144 | tf_op jit(solution)/shard_map/all_to_all | solution.py:591
  130.2 0.0 copy-done
  130.2 2.0 %solve.1 = (f32[48,128]{1,0:T(8,128)}, f32[48,128]{1,0:T(8,128)}) custom-call(f32[256,128]{1,0:T(8,128)S(1)} %bitcast.19, f32[1,128]{1,0:T(1,128)S(1)} %get-tuple-element.53.state_ref, f32[48,128]{1,0:T(8,128)S(1)} %bitcast.23, f32[4,48,128]{2,1,0:T(8,128)S(1)} %get-tuple-element.54.v_ref, f32[4,48,128]{2,1,0:T(8,128)S(1)} %get-tuple-element.55.z_ref), custom_call_target="tpu_custom_call" | custom-call | tf_op jit(solution)/shard_map/solve/pallas_call | solution.py:592
Async XLA Ops:
  0.6 34.9 %copy-start.4 = (f32[3,16]{1,0:T(4,128)S(1)}, f32[3,16]{1,0:T(4,128)}, u32[]{:S(2)}) copy-start(f32[3,16]{1,0:T(4,128)} %refs_5_.1) | copy-start | bytes 580
  0.6 34.9 %copy-start.3 = (f32[128]{0:T(128)S(1)}, f32[128]{0:T(128)}, u32[]{:S(2)}) copy-start(f32[128]{0:T(128)} %param.12) | copy-start | bytes 1540
  0.7 34.9 %copy-start.2 = (f32[128]{0:T(128)S(1)}, f32[128]{0:T(128)}, u32[]{:S(2)}) copy-start(f32[128]{0:T(128)} %param.13) | copy-start | bytes 1540
  0.7 34.9 %copy-start.1 = (f32[16]{0:T(128)S(1)}, f32[16]{0:T(128)}, u32[]{:S(2)}) copy-start(f32[16]{0:T(128)} %param.10) | copy-start | bytes 196
  2.2 15.9 %all-to-all-start = ((f32[8,8,128]{2,1,0:T(8,128)}), f32[8,8,128]{2,1,0:T(8,128)S(1)}, u32[]{:S(2)}, u32[]{:S(2)}) async-start(f32[8,8,128]{2,1,0:T(8,128)} %get-tuple-element.30), calls=%async_computation | async-start | bytes 65536 | tf_op jit(solution)/shard_map/all_to_all | solution.py:509
  16.8 25.2 %copy-start.5 = (s32[32]{0:T(128)}, s32[32]{0:T(128)S(1)}, u32[]{:S(2)}) copy-start(s32[32]{0:T(128)S(1)} %get-tuple-element.34.table_hbm) | copy-start | bytes 388
  37.5 11.4 %all-to-all-start.2 = ((f32[8,8,128]{2,1,0:T(8,128)}), f32[8,8,128]{2,1,0:T(8,128)S(1)}, u32[]{:S(2)}, u32[]{:S(2)}) async-start(f32[8,8,128]{2,1,0:T(8,128)} %get-tuple-element.33), calls=%async_computation.2 | async-start | bytes 65536 | tf_op jit(solution)/shard_map/all_to_all | solution.py:509
  62.9 10.2 %all-to-all-start.4 = ((f32[8,8,128]{2,1,0:T(8,128)}), f32[8,8,128]{2,1,0:T(8,128)S(1)}, u32[]{:S(2)}, u32[]{:S(2)}) async-start(f32[8,8,128]{2,1,0:T(8,128)} %get-tuple-element.42), calls=%async_computation.4 | async-start | bytes 65536 | tf_op jit(solution)/shard_map/all_to_all | solution.py:509
  70.6 59.5 %copy-start = (f32[3,16,128]{2,1,0:T(8,128)S(1)}, f32[3,16,128]{2,1,0:T(8,128)}, u32[]{:S(2)}) copy-start(f32[3,16,128]{2,1,0:T(8,128)} %param.9) | copy-start | bytes 73732
  87.2 10.3 %all-to-all-start.6 = ((f32[8,8,128]{2,1,0:T(8,128)}), f32[8,8,128]{2,1,0:T(8,128)S(1)}, u32[]{:S(2)}, u32[]{:S(2)}) async-start(f32[8,8,128]{2,1,0:T(8,128)} %get-tuple-element.47), calls=%async_computation.6 | async-start | bytes 65536 | tf_op jit(solution)/shard_map/all_to_all | solution.py:509

commit v4 on v3

--- a/solution.py
+++ b/solution.py
@@ -81,7 +81,7 @@
 
 
 def pick(row, lane):
-    return row[:, lane:lane + 1]
+    return jnp.broadcast_to(row[:, lane:lane + 1], row.shape)
 
 
 def pack(entries):
@@ -306,7 +306,7 @@
         meta = jnp.dot(chosen, arrived, preferred_element_type=F32)
         eye = lax.broadcasted_iota(jnp.int32, (sources, sources), 0) == lane_iota((sources, sources))
         named = [
-            jnp.sum(jnp.where(eye, pick(meta, rank), 0.0), axis=0, keepdims=True) for rank in range(CAPD)
+            jnp.sum(jnp.where(eye, meta[:, rank:rank + 1], 0.0), axis=0, keepdims=True) for rank in range(CAPD)
         ]
         named = jnp.concatenate(
             [jnp.broadcast_to(n, (TILE, sources)) for n in named], axis=0
@@ -438,7 +438,8 @@
     square = sum(entry * entry for entry in vector)
     size = jnp.sqrt(square)
     weights.append(size)
-    return weights, [entry / size for entry in vector]
+    inverse = 1.0 / size
+    return weights, [entry * inverse for entry in vector]
 
 
 def solve_kernel(rows_ref, state_ref, f_ref, v_ref, z_ref, solution_ref, residual_ref):
@@ -458,12 +459,13 @@
         weights, unit = orthogonalized(vector, units, k + 2)
         units.append(unit)
         triangle.update({(e, k): weights[e] for e in range(k + 1)})
+    inverses = [1.0 / triangle[k, k] for k in range(ITERS)]
     answers = [None] * ITERS
     for k in reversed(range(ITERS)):
         running = beta * units[k][0]
         for later in reversed(range(k + 1, ITERS)):
             running = running - triangle[k, later] * answers[later]
-        answers[k] = running / triangle[k, k]
+        answers[k] = running * inverses[k]
     result = answers[0] * v_ref[0]
     rest = f_ref[...] - answers[0] * z_ref[0]
     for k in range(1, ITERS):

time: 133 us -> 131 us (0.985)
  Pallas kernels: 27.7 us -> 26.2 us
where the time goes in v4:
time: 131 us
  blocking collectives  73.9 us (56%)
  Pallas kernels  26.2 us (20%)
  starting transfers between devices  20.2 us (15%)
  waiting for transfers between devices  8.89 us (7%)
  between operations  1.42 us (1%)
    all_to_all x4, blocking collectives, exchange(): recv = lax.all_to_all(out, 'col', split_axis=0, concat_axis=0, tiled=True)  55.2 us
    all_to_all x4, starting transfers between devices, exchange(): lax.all_to_all(send, 'row', split_axis=0, concat_axis=0, tiled=True)  20.2 us
    all_to_all x1, blocking collectives, on_device(): lax.all_to_all(send, ('row', 'col'), split_axis=0, concat_axis=0, tiled=T...  18.7 us
    pallas_call x4, Pallas kernels, exchange(): pl.pallas_call(functools.partial(near_kernel, comps, cil, first), out_sha...  18 us
    all_to_all x4, waiting for transfers between devices, exchange(): lax.all_to_all(send, 'row', split_axis=0, concat_axis=0, tiled=True)  8.89 us
    pallas_call x4, Pallas kernels, on_device(): pl.pallas_call(functools.partial(krylov_kernel, comps, cil, cols, total,...  5.54 us
  transfers between devices with their start and end apart: 4, of which 4 were waited for; matrix products, arithmetic and copies ran while one was open for 0% of the time, Pallas kernels for 14%

profile of v4, /device:TPU:1, one launch (start us, length us, event | category | flops | bytes accessed | tf_op | source)
XLA Modules:
  0.0 130.6 jit_solution(2265405279195247594)
XLA Ops:
  0.6 0.0 copy-start.4
  0.6 0.0 copy-start.3
  0.7 0.0 copy-start.2
  0.7 0.0 copy-start.1
  0.7 1.5 %first.1 = (f32[8,8,128]{2,1,0:T(8,128)}, f32[48,128]{1,0:T(8,128)S(1)}) custom-call(f32[48,128]{1,0:T(8,128)} %bitcast.22, f32[3,16]{1,0:T(4,128)} %refs_5_.1, f32[1,128]{1,0:T(1,128)} %bitcast.32), custom_call_target="tpu_custom_call" | custom-call | tf_op jit(solution)/shard_map/first/pallas_call | solution.py:546
  2.2 9.0 %all-to-all-start = ((f32[8,8,128]{2,1,0:T(8,128)}), f32[8,8,128]{2,1,0:T(8,128)S(1)}, u32[]{:S(2)}, u32[]{:S(2)}) async-start(f32[8,8,128]{2,1,0:T(8,128)} %get-tuple-element.30), calls=%async_computation | async-start | bytes 65536 | tf_op jit(solution)/shard_map/all_to_all | solution.py:511
  11.9 4.9 %near.4 = (bf16[32,8,128]{2,1,0:T(8,128)(2,1)S(1)}, bf16[6,384,384]{2,1,0:T(8,128)(2,1)S(1)}, s32[32]{0:T(128)S(1)}) custom-call(s32[2,32]{1,0:T(2,128)} %bitcast.36, s32[32]{0:T(128)} %bitcast.40, s32[1]{0:T(128)S(6)} %copy.12.count_ref, f32[48,128]{1,0:T(8,128)S(1)} %get-tuple-element.31.x_ref.refs_1_, bf16[32,384,384]{2,1,0:T(8,128)(2,1)} %b_ref.7), custom_call_target="tpu_custom_call" | custom-call | tf_op jit(solution)/shard_map/near/pallas_call | solution.py:519
  16.8 0.0 copy-start.5
  16.8 1.3 all-to-all-done.rows_ref
  18.1 0.1 join.4
  18.2 17.3 %all_to_all.51 = bf16[32,24,128]{2,1,0:T(8,128)(2,1)S(1)} all-to-all(bf16[32,24,128]{2,1,0:T(8,128)(2,1)S(1)} %join.4), channel_id=1, replica_groups=mesh['row'=8,'col'=32] {'col'}, dimensions={0} | all-to-all | bytes 393216 | tf_op jit(solution)/shard_map/all_to_all | solution.py:543
  35.5 0.0 copy-done.4
  35.5 0.0 copy-done.3
  35.5 0.0 copy-done.2
  35.5 0.0 copy-done.1
  35.5 2.0 %krylov.4 = (bf16[152,512]{1,0:T(8,128)(2,1)S(1)}, f32[4,32,16,128]{3,2,1,0:T(8,128)S(1)}, f32[8,8,128]{2,1,0:T(8,128)}, f32[48,128]{1,0:T(8,128)S(1)}, f32[1,48...) custom-call(bf16[768,128]{1,0:T(8,128)(2,1)S(1)} %bitcast.16, ...), custom_call_target="tpu_custom_call" | custom-call | tf_op jit(solution)/shard_map/krylov/pallas_call | solution.py:580
  37.5 4.5 %all-to-all-start.2 = ((f32[8,8,128]{2,1,0:T(8,128)}), f32[8,8,128]{2,1,0:T(8,128)S(1)}, u32[]{:S(2)}, u32[]{:S(2)}) async-start(f32[8,8,128]{2,1,0:T(8,128)} %get-tuple-element.33), calls=%async_computation.2 | async-start | bytes 65536 | tf_op jit(solution)/shard_map/all_to_all | solution.py:511
  42.0 0.0 copy-done.5
  42.0 4.4 %near.5.near_ref = bf16[32,8,128]{2,1,0:T(8,128)(2,1)S(1)} custom-call(s32[2,32]{1,0:T(2,128)} %bitcast.37, s32[32]{0:T(128)} %copy-done.5, s32[1]{0:T(128)S(6)} %copy.12.count_ref, f32[48,128]{1,0:T(8,128)S(1)} %get-tuple-element.35.x_ref.refs_1_, bf16[32,384,384]{2,1,0:T(8,128)(2,1)} %b_ref.7, bf16[6,384,384]{2,1,0:T(8,128)(2,1)S(1)} %get-tuple-element.36.refs_0_), custom_call_target="tpu_custom_call" | custom-call | tf_op jit(solution)/shard_map/near/pallas_call | solution.py:519
  46.4 2.5 %all-to-all-done.2.rows_ref = f32[8,8,128]{2,1,0:T(8,128)S(1)} async-done(((f32[8,8,128]{2,1,0:T(8,128)}), f32[8,8,128]{2,1,0:T(8,128)S(1)}, u32[]{:S(2)}, u32[]{:S(2)}) %all-to-all-start.2) | async-done | bytes 32800 | tf_op jit(solution)/shard_map/all_to_all | solution.py:511
  48.9 0.1 join.5
  49.0 12.7 %all_to_all.52 = bf16[32,16,128]{2,1,0:T(8,128)(2,1)S(1)} all-to-all(bf16[32,16,128]{2,1,0:T(8,128)(2,1)S(1)} %join.5), channel_id=1, replica_groups=mesh['row'=8,'col'=32] {'col'}, dimensions={0} | all-to-all | bytes 262144 | tf_op jit(solution)/shard_map/all_to_all | solution.py:543
  61.6 1.2 krylov.5
  62.9 3.3 %all-to-all-start.4 = ((f32[8,8,128]{2,1,0:T(8,128)}), f32[8,8,128]{2,1,0:T(8,128)S(1)}, u32[]{:S(2)}, u32[]{:S(2)}) async-start(f32[8,8,128]{2,1,0:T(8,128)} %get-tuple-element.42), calls=%async_computation.4 | async-start | bytes 65536 | tf_op jit(solution)/shard_map/all_to_all | solution.py:511
  66.2 4.4 %near.6.near_ref = bf16[32,8,128]{2,1,0:T(8,128)(2,1)S(1)} custom-call(s32[2,32]{1,0:T(2,128)} %bitcast.38, s32[32]{0:T(128)} %copy-done.5, s32[1]{0:T(128)S(6)} %copy.12.count_ref, f32[48,128]{1,0:T(8,128)S(1)} %get-tuple-element.43.x_ref.refs_1_, bf16[32,384,384]{2,1,0:T(8,128)(2,1)} %b_ref.7, bf16[6,384,384]{2,1,0:T(8,128)(2,1)S(1)} %get-tuple-element.36.refs_0_), custom_call_target="tpu_custom_call" | custom-call | tf_op jit(solution)/shard_map/near/pallas_call | solution.py:519
  70.6 0.0 copy-start
  70.6 2.5 %all-to-all-done.4.rows_ref = f32[8,8,128]{2,1,0:T(8,128)S(1)} async-done(((f32[8,8,128]{2,1,0:T(8,128)}), f32[8,8,128]{2,1,0:T(8,128)S(1)}, u32[]{:S(2)}, u32[]{:S(2)}) %all-to-all-start.4) | async-done | bytes 32800 | tf_op jit(solution)/shard_map/all_to_all | solution.py:511
  73.1 0.1 join.6
  73.2 12.6 %all_to_all.53 = bf16[32,16,128]{2,1,0:T(8,128)(2,1)S(1)} all-to-all(bf16[32,16,128]{2,1,0:T(8,128)(2,1)S(1)} %join.6), channel_id=1, replica_groups=mesh['row'=8,'col'=32] {'col'}, dimensions={0} | all-to-all | bytes 262144 | tf_op jit(solution)/shard_map/all_to_all | solution.py:543
  85.8 1.2 krylov.6
  87.0 3.3 %all-to-all-start.6 = ((f32[8,8,128]{2,1,0:T(8,128)}), f32[8,8,128]{2,1,0:T(8,128)S(1)}, u32[]{:S(2)}, u32[]{:S(2)}) async-start(f32[8,8,128]{2,1,0:T(8,128)} %get-tuple-element.47), calls=%async_computation.6 | async-start | bytes 65536 | tf_op jit(solution)/shard_map/all_to_all | solution.py:511
  90.4 4.4 %near.7.near_ref = bf16[32,8,128]{2,1,0:T(8,128)(2,1)S(1)} custom-call(s32[2,32]{1,0:T(2,128)} %bitcast.39, s32[32]{0:T(128)} %copy-done.5, s32[1]{0:T(128)S(6)} %copy.12.count_ref, f32[48,128]{1,0:T(8,128)S(1)} %get-tuple-element.48.x_ref.refs_1_, bf16[32,384,384]{2,1,0:T(8,128)(2,1)} %b_ref.7, bf16[6,384,384]{2,1,0:T(8,128)(2,1)S(1)} %get-tuple-element.36.refs_0_), custom_call_target="tpu_custom_call" | custom-call | tf_op jit(solution)/shard_map/near/pallas_call | solution.py:519
  94.8 2.6 %all-to-all-done.6.rows_ref = f32[8,8,128]{2,1,0:T(8,128)S(1)} async-done(((f32[8,8,128]{2,1,0:T(8,128)}), f32[8,8,128]{2,1,0:T(8,128)S(1)}, u32[]{:S(2)}, u32[]{:S(2)}) %all-to-all-start.6) | async-done | bytes 32800 | tf_op jit(solution)/shard_map/all_to_all | solution.py:511
  97.3 0.1 join.7
  97.4 12.6 %all_to_all.54 = bf16[32,16,128]{2,1,0:T(8,128)(2,1)S(1)} all-to-all(bf16[32,16,128]{2,1,0:T(8,128)(2,1)S(1)} %join.7), channel_id=1, replica_groups=mesh['row'=8,'col'=32] {'col'}, dimensions={0} | all-to-all | bytes 262144 | tf_op jit(solution)/shard_map/all_to_all | solution.py:543
  110.0 1.1 krylov.7
  111.1 18.7 %all_to_all.55 = f32[256,1,128]{2,1,0:T(1,128)S(1)} all-to-all(f32[256,1,128]{2,1,0:T(1,128)S(1)} %bitcast.21), channel_id=1, replica_groups=mesh['row'=8,'col'=32] {'row','col'}, dimensions={0} | all-to-all | bytes 262144 | tf_op jit(solution)/shard_map/all_to_all | solution.py:593
  129.9 0.0 copy-done
  129.9 0.8 solve.1
Async XLA Ops:
  0.6 34.9 %copy-start.4 = (f32[3,16]{1,0:T(4,128)S(1)}, f32[3,16]{1,0:T(4,128)}, u32[]{:S(2)}) copy-start(f32[3,16]{1,0:T(4,128)} %refs_5_.1) | copy-start | bytes 580
  0.6 34.9 %copy-start.3 = (f32[128]{0:T(128)S(1)}, f32[128]{0:T(128)}, u32[]{:S(2)}) copy-start(f32[128]{0:T(128)} %param.12) | copy-start | bytes 1540
  0.7 34.9 %copy-start.2 = (f32[128]{0:T(128)S(1)}, f32[128]{0:T(128)}, u32[]{:S(2)}) copy-start(f32[128]{0:T(128)} %param.13) | copy-start | bytes 1540
  0.7 34.9 %copy-start.1 = (f32[16]{0:T(128)S(1)}, f32[16]{0:T(128)}, u32[]{:S(2)}) copy-start(f32[16]{0:T(128)} %param.10) | copy-start | bytes 196
  2.2 15.9 %all-to-all-start = ((f32[8,8,128]{2,1,0:T(8,128)}), f32[8,8,128]{2,1,0:T(8,128)S(1)}, u32[]{:S(2)}, u32[]{:S(2)}) async-start(f32[8,8,128]{2,1,0:T(8,128)} %get-tuple-element.30), calls=%async_computation | async-start | bytes 65536 | tf_op jit(solution)/shard_map/all_to_all | solution.py:511
  16.8 25.2 %copy-start.5 = (s32[32]{0:T(128)}, s32[32]{0:T(128)S(1)}, u32[]{:S(2)}) copy-start(s32[32]{0:T(128)S(1)} %get-tuple-element.34.table_hbm) | copy-start | bytes 388
  37.5 11.4 %all-to-all-start.2 = ((f32[8,8,128]{2,1,0:T(8,128)}), f32[8,8,128]{2,1,0:T(8,128)S(1)}, u32[]{:S(2)}, u32[]{:S(2)}) async-start(f32[8,8,128]{2,1,0:T(8,128)} %get-tuple-element.33), calls=%async_computation.2 | async-start | bytes 65536 | tf_op jit(solution)/shard_map/all_to_all | solution.py:511
  62.9 10.3 %all-to-all-start.4 = ((f32[8,8,128]{2,1,0:T(8,128)}), f32[8,8,128]{2,1,0:T(8,128)S(1)}, u32[]{:S(2)}, u32[]{:S(2)}) async-start(f32[8,8,128]{2,1,0:T(8,128)} %get-tuple-element.42), calls=%async_computation.4 | async-start | bytes 65536 | tf_op jit(solution)/shard_map/all_to_all | solution.py:511
  70.6 59.3 %copy-start = (f32[3,16,128]{2,1,0:T(8,128)S(1)}, f32[3,16,128]{2,1,0:T(8,128)}, u32[]{:S(2)}) copy-start(f32[3,16,128]{2,1,0:T(8,128)} %param.9) | copy-start | bytes 73732
  87.0 10.3 %all-to-all-start.6 = ((f32[8,8,128]{2,1,0:T(8,128)}), f32[8,8,128]{2,1,0:T(8,128)S(1)}, u32[]{:S(2)}, u32[]{:S(2)}) async-start(f32[8,8,128]{2,1,0:T(8,128)} %get-tuple-element.47), calls=%async_computation.6 | async-start | bytes 65536 | tf_op jit(solution)/shard_map/all_to_all | solution.py:511

commit v5 on v4

--- a/solution.py
+++ b/solution.py
@@ -571,7 +571,7 @@
                 struct(1 + comps, cols, cil, LANES),
             ]
         outs += [
-            struct(rows * cols, LANES) if last else struct(rows, TILE, LANES),
+            struct(rows * cols, LANES) if last else struct(rows, comps + 1, LANES),
             struct(flat, points),
             struct(step, flat, points),
             struct(step, flat, points),

time: 131 us -> 131 us (level)
  no operation moved by 1% of the time
where the time goes in v5:
time: 131 us
  blocking collectives  74.4 us (57%)
  Pallas kernels  26.2 us (20%)
  starting transfers between devices  20.6 us (16%)
  waiting for transfers between devices  8.07 us (6%)
  between operations  1.4 us (1%)
    all_to_all x4, blocking collectives, exchange(): recv = lax.all_to_all(out, 'col', split_axis=0, concat_axis=0, tiled=True)  55.4 us
    all_to_all x4, starting transfers between devices, exchange(): lax.all_to_all(send, 'row', split_axis=0, concat_axis=0, tiled=True)  20.6 us
    all_to_all x1, blocking collectives, on_device(): lax.all_to_all(send, ('row', 'col'), split_axis=0, concat_axis=0, tiled=T...  19 us
    pallas_call x4, Pallas kernels, exchange(): pl.pallas_call(functools.partial(near_kernel, comps, cil, first), out_sha...  18 us
    all_to_all x4, waiting for transfers between devices, exchange(): lax.all_to_all(send, 'row', split_axis=0, concat_axis=0, tiled=True)  8.07 us
    pallas_call x4, Pallas kernels, on_device(): pl.pallas_call(functools.partial(krylov_kernel, comps, cil, cols, total,...  5.53 us
  transfers between devices with their start and end apart: 4, of which 4 were waited for; matrix products, arithmetic and copies ran while one was open for 0% of the time, Pallas kernels for 14%

profile of v5, /device:TPU:1, one launch (start us, length us, event | category | flops | bytes accessed | tf_op | source)
XLA Modules:
  0.0 130.6 jit_solution(5052354472406018965)
XLA Ops:
  0.6 0.0 copy-start.4
  0.6 0.0 copy-start.3
  0.7 0.0 copy-start.2
  0.7 0.0 copy-start.1
  0.7 1.5 %first.1 = (f32[8,8,128]{2,1,0:T(8,128)}, f32[48,128]{1,0:T(8,128)S(1)}) custom-call(f32[48,128]{1,0:T(8,128)} %bitcast.22, f32[3,16]{1,0:T(4,128)} %refs_5_.1, f32[1,128]{1,0:T(1,128)} %bitcast.32), custom_call_target="tpu_custom_call" | custom-call | tf_op jit(solution)/shard_map/first/pallas_call | solution.py:546
  2.2 9.0 %all-to-all-start = ((f32[8,8,128]{2,1,0:T(8,128)}), f32[8,8,128]{2,1,0:T(8,128)S(1)}, u32[]{:S(2)}, u32[]{:S(2)}) async-start(f32[8,8,128]{2,1,0:T(8,128)} %get-tuple-element.30), calls=%async_computation | async-start | bytes 65536 | tf_op jit(solution)/shard_map/all_to_all | solution.py:511
  11.9 4.9 %near.4 = (bf16[32,8,128]{2,1,0:T(8,128)(2,1)S(1)}, bf16[6,384,384]{2,1,0:T(8,128)(2,1)S(1)}, s32[32]{0:T(128)S(1)}) custom-call(s32[2,32]{1,0:T(2,128)} %bitcast.36, s32[32]{0:T(128)} %bitcast.40, s32[1]{0:T(128)S(6)} %copy.12.count_ref, f32[48,128]{1,0:T(8,128)S(1)} %get-tuple-element.31.x_ref.refs_1_, bf16[32,384,384]{2,1,0:T(8,128)(2,1)} %b_ref.7), custom_call_target="tpu_custom_call" | custom-call | tf_op jit(solution)/shard_map/near/pallas_call | solution.py:519
  16.8 0.0 copy-start.5
  16.8 1.3 all-to-all-done.rows_ref
  18.1 0.1 join.4
  18.2 17.3 %all_to_all.51 = bf16[32,24,128]{2,1,0:T(8,128)(2,1)S(1)} all-to-all(bf16[32,24,128]{2,1,0:T(8,128)(2,1)S(1)} %join.4), channel_id=1, replica_groups=mesh['row'=8,'col'=32] {'col'}, dimensions={0} | all-to-all | bytes 393216 | tf_op jit(solution)/shard_map/all_to_all | solution.py:543
  35.5 0.0 copy-done.4
  35.5 0.0 copy-done.3
  35.5 0.0 copy-done.2
  35.5 0.0 copy-done.1
  35.5 2.0 %krylov.4 = (bf16[152,512]{1,0:T(8,128)(2,1)S(1)}, f32[4,32,16,128]{3,2,1,0:T(8,128)S(1)}, f32[8,4,128]{2,1,0:T(4,128)}, f32[48,128]{1,0:T(8,128)S(1)}, f32[1,48...) custom-call(bf16[768,128]{1,0:T(8,128)(2,1)S(1)} %bitcast.16, ...), custom_call_target="tpu_custom_call" | custom-call | tf_op jit(solution)/shard_map/krylov/pallas_call | solution.py:580
  37.5 4.5 %all-to-all-start.2 = ((f32[8,4,128]{2,1,0:T(4,128)}), f32[8,4,128]{2,1,0:T(4,128)S(1)}, u32[]{:S(2)}, u32[]{:S(2)}) async-start(f32[8,4,128]{2,1,0:T(4,128)} %get-tuple-element.33), calls=%async_computation.2 | async-start | bytes 32768 | tf_op jit(solution)/shard_map/all_to_all | solution.py:511
  42.0 0.0 copy-done.5
  42.0 4.4 %near.5.near_ref = bf16[32,8,128]{2,1,0:T(8,128)(2,1)S(1)} custom-call(s32[2,32]{1,0:T(2,128)} %bitcast.37, s32[32]{0:T(128)} %copy-done.5, s32[1]{0:T(128)S(6)} %copy.12.count_ref, f32[48,128]{1,0:T(8,128)S(1)} %get-tuple-element.35.x_ref.refs_1_, bf16[32,384,384]{2,1,0:T(8,128)(2,1)} %b_ref.7, bf16[6,384,384]{2,1,0:T(8,128)(2,1)S(1)} %get-tuple-element.36.refs_0_), custom_call_target="tpu_custom_call" | custom-call | tf_op jit(solution)/shard_map/near/pallas_call | solution.py:519
  46.3 2.3 %all-to-all-done.2.rows_ref = f32[8,4,128]{2,1,0:T(4,128)S(1)} async-done(((f32[8,4,128]{2,1,0:T(4,128)}), f32[8,4,128]{2,1,0:T(4,128)S(1)}, u32[]{:S(2)}, u32[]{:S(2)}) %all-to-all-start.2) | async-done | bytes 16416 | tf_op jit(solution)/shard_map/all_to_all | solution.py:511
  48.6 0.1 join.5
  48.7 12.7 %all_to_all.52 = bf16[32,16,128]{2,1,0:T(8,128)(2,1)S(1)} all-to-all(bf16[32,16,128]{2,1,0:T(8,128)(2,1)S(1)} %join.5), channel_id=1, replica_groups=mesh['row'=8,'col'=32] {'col'}, dimensions={0} | all-to-all | bytes 262144 | tf_op jit(solution)/shard_map/all_to_all | solution.py:543
  61.4 1.2 krylov.5
  62.6 3.5 %all-to-all-start.4 = ((f32[8,4,128]{2,1,0:T(4,128)}), f32[8,4,128]{2,1,0:T(4,128)S(1)}, u32[]{:S(2)}, u32[]{:S(2)}) async-start(f32[8,4,128]{2,1,0:T(4,128)} %get-tuple-element.42), calls=%async_computation.4 | async-start | bytes 32768 | tf_op jit(solution)/shard_map/all_to_all | solution.py:511
  66.1 4.4 %near.6.near_ref = bf16[32,8,128]{2,1,0:T(8,128)(2,1)S(1)} custom-call(s32[2,32]{1,0:T(2,128)} %bitcast.38, s32[32]{0:T(128)} %copy-done.5, s32[1]{0:T(128)S(6)} %copy.12.count_ref, f32[48,128]{1,0:T(8,128)S(1)} %get-tuple-element.43.x_ref.refs_1_, bf16[32,384,384]{2,1,0:T(8,128)(2,1)} %b_ref.7, bf16[6,384,384]{2,1,0:T(8,128)(2,1)S(1)} %get-tuple-element.36.refs_0_), custom_call_target="tpu_custom_call" | custom-call | tf_op jit(solution)/shard_map/near/pallas_call | solution.py:519
  70.5 0.0 copy-start
  70.5 2.2 %all-to-all-done.4.rows_ref = f32[8,4,128]{2,1,0:T(4,128)S(1)} async-done(((f32[8,4,128]{2,1,0:T(4,128)}), f32[8,4,128]{2,1,0:T(4,128)S(1)}, u32[]{:S(2)}, u32[]{:S(2)}) %all-to-all-start.4) | async-done | bytes 16416 | tf_op jit(solution)/shard_map/all_to_all | solution.py:511
  72.7 0.1 join.6
  72.8 12.7 %all_to_all.53 = bf16[32,16,128]{2,1,0:T(8,128)(2,1)S(1)} all-to-all(bf16[32,16,128]{2,1,0:T(8,128)(2,1)S(1)} %join.6), channel_id=1, replica_groups=mesh['row'=8,'col'=32] {'col'}, dimensions={0} | all-to-all | bytes 262144 | tf_op jit(solution)/shard_map/all_to_all | solution.py:543
  85.6 1.2 krylov.6
  86.8 3.5 %all-to-all-start.6 = ((f32[8,4,128]{2,1,0:T(4,128)}), f32[8,4,128]{2,1,0:T(4,128)S(1)}, u32[]{:S(2)}, u32[]{:S(2)}) async-start(f32[8,4,128]{2,1,0:T(4,128)} %get-tuple-element.47), calls=%async_computation.6 | async-start | bytes 32768 | tf_op jit(solution)/shard_map/all_to_all | solution.py:511
  90.3 4.4 %near.7.near_ref = bf16[32,8,128]{2,1,0:T(8,128)(2,1)S(1)} custom-call(s32[2,32]{1,0:T(2,128)} %bitcast.39, s32[32]{0:T(128)} %copy-done.5, s32[1]{0:T(128)S(6)} %copy.12.count_ref, f32[48,128]{1,0:T(8,128)S(1)} %get-tuple-element.48.x_ref.refs_1_, bf16[32,384,384]{2,1,0:T(8,128)(2,1)} %b_ref.7, bf16[6,384,384]{2,1,0:T(8,128)(2,1)S(1)} %get-tuple-element.36.refs_0_), custom_call_target="tpu_custom_call" | custom-call | tf_op jit(solution)/shard_map/near/pallas_call | solution.py:519
  94.7 2.3 %all-to-all-done.6.rows_ref = f32[8,4,128]{2,1,0:T(4,128)S(1)} async-done(((f32[8,4,128]{2,1,0:T(4,128)}), f32[8,4,128]{2,1,0:T(4,128)S(1)}, u32[]{:S(2)}, u32[]{:S(2)}) %all-to-all-start.6) | async-done | bytes 16416 | tf_op jit(solution)/shard_map/all_to_all | solution.py:511
  96.9 0.1 join.7
  97.0 12.7 %all_to_all.54 = bf16[32,16,128]{2,1,0:T(8,128)(2,1)S(1)} all-to-all(bf16[32,16,128]{2,1,0:T(8,128)(2,1)S(1)} %join.7), channel_id=1, replica_groups=mesh['row'=8,'col'=32] {'col'}, dimensions={0} | all-to-all | bytes 262144 | tf_op jit(solution)/shard_map/all_to_all | solution.py:543
  109.8 1.1 krylov.7
  110.9 19.0 %all_to_all.55 = f32[256,1,128]{2,1,0:T(1,128)S(1)} all-to-all(f32[256,1,128]{2,1,0:T(1,128)S(1)} %bitcast.21), channel_id=1, replica_groups=mesh['row'=8,'col'=32] {'row','col'}, dimensions={0} | all-to-all | bytes 262144 | tf_op jit(solution)/shard_map/all_to_all | solution.py:593
  129.8 0.0 copy-done
  129.8 0.8 solve.1
Async XLA Ops:
  0.6 34.9 %copy-start.4 = (f32[3,16]{1,0:T(4,128)S(1)}, f32[3,16]{1,0:T(4,128)}, u32[]{:S(2)}) copy-start(f32[3,16]{1,0:T(4,128)} %refs_5_.1) | copy-start | bytes 580
  0.6 34.9 %copy-start.3 = (f32[128]{0:T(128)S(1)}, f32[128]{0:T(128)}, u32[]{:S(2)}) copy-start(f32[128]{0:T(128)} %param.12) | copy-start | bytes 1540
  0.7 34.9 %copy-start.2 = (f32[128]{0:T(128)S(1)}, f32[128]{0:T(128)}, u32[]{:S(2)}) copy-start(f32[128]{0:T(128)} %param.13) | copy-start | bytes 1540
  0.7 34.9 %copy-start.1 = (f32[16]{0:T(128)S(1)}, f32[16]{0:T(128)}, u32[]{:S(2)}) copy-start(f32[16]{0:T(128)} %param.10) | copy-start | bytes 196
  2.2 15.9 %all-to-all-start = ((f32[8,8,128]{2,1,0:T(8,128)}), f32[8,8,128]{2,1,0:T(8,128)S(1)}, u32[]{:S(2)}, u32[]{:S(2)}) async-start(f32[8,8,128]{2,1,0:T(8,128)} %get-tuple-element.30), calls=%async_computation | async-start | bytes 65536 | tf_op jit(solution)/shard_map/all_to_all | solution.py:511
  16.8 25.2 %copy-start.5 = (s32[32]{0:T(128)}, s32[32]{0:T(128)S(1)}, u32[]{:S(2)}) copy-start(s32[32]{0:T(128)S(1)} %get-tuple-element.34.table_hbm) | copy-start | bytes 388
  37.5 11.1 %all-to-all-start.2 = ((f32[8,4,128]{2,1,0:T(4,128)}), f32[8,4,128]{2,1,0:T(4,128)S(1)}, u32[]{:S(2)}, u32[]{:S(2)}) async-start(f32[8,4,128]{2,1,0:T(4,128)} %get-tuple-element.33), calls=%async_computation.2 | async-start | bytes 32768 | tf_op jit(solution)/shard_map/all_to_all | solution.py:511
  62.6 10.2 %all-to-all-start.4 = ((f32[8,4,128]{2,1,0:T(4,128)}), f32[8,4,128]{2,1,0:T(4,128)S(1)}, u32[]{:S(2)}, u32[]{:S(2)}) async-start(f32[8,4,128]{2,1,0:T(4,128)} %get-tuple-element.42), calls=%async_computation.4 | async-start | bytes 32768 | tf_op jit(solution)/shard_map/all_to_all | solution.py:511
  70.5 59.4 %copy-start = (f32[3,16,128]{2,1,0:T(8,128)S(1)}, f32[3,16,128]{2,1,0:T(8,128)}, u32[]{:S(2)}) copy-start(f32[3,16,128]{2,1,0:T(8,128)} %param.9) | copy-start | bytes 73732
  86.8 10.2 %all-to-all-start.6 = ((f32[8,4,128]{2,1,0:T(4,128)}), f32[8,4,128]{2,1,0:T(4,128)S(1)}, u32[]{:S(2)}, u32[]{:S(2)}) async-start(f32[8,4,128]{2,1,0:T(4,128)} %get-tuple-element.47), calls=%async_computation.6 | async-start | bytes 32768 | tf_op jit(solution)/shard_map/all_to_all | solution.py:511

commit v6 on v4

--- a/solution.py
+++ b/solution.py
@@ -113,7 +113,7 @@
 
 TILE = 8
 KEPT = 6
-CHUNKS = (8, 8, 8, 8)
+CHUNKS = (8, 12, 12)
 META = 6
 DOTS = 14
 PITCH = {True: 24, False: 16}

time: 131 us -> 132 us (level)
  no operation moved by 1% of the time
where the time goes in v6:
time: 132 us
  blocking collectives  74.1 us (56%)
  Pallas kernels  27.1 us (21%)
  starting transfers between devices  20.8 us (16%)
  waiting for transfers between devices  8.07 us (6%)
  between operations  1.4 us (1%)
    all_to_all x4, blocking collectives, exchange(): recv = lax.all_to_all(out, 'col', split_axis=0, concat_axis=0, tiled=True)  55.2 us
    all_to_all x4, starting transfers between devices, exchange(): lax.all_to_all(send, 'row', split_axis=0, concat_axis=0, tiled=True)  20.8 us
    pallas_call x4, Pallas kernels, exchange(): pl.pallas_call(functools.partial(near_kernel, comps, cil, first), out_sha...  18.9 us
    all_to_all x1, blocking collectives, on_device(): lax.all_to_all(send, ('row', 'col'), split_axis=0, concat_axis=0, tiled=T...  18.9 us
    all_to_all x4, waiting for transfers between devices, exchange(): lax.all_to_all(send, 'row', split_axis=0, concat_axis=0, tiled=True)  8.07 us
    pallas_call x4, Pallas kernels, on_device(): pl.pallas_call(functools.partial(krylov_kernel, comps, cil, cols, total,...  5.55 us
  transfers between devices with their start and end apart: 4, of which 4 were waited for; matrix products, arithmetic and copies ran while one was open for 0% of the time, Pallas kernels for 14%

profile of v6, /device:TPU:1, one launch (start us, length us, event | category | flops | bytes accessed | tf_op | source)
XLA Modules:
  0.0 131.6 jit_solution(945144850039193702)
XLA Ops:
  0.6 0.0 copy-start.4
  0.6 0.0 copy-start.3
  0.7 0.0 copy-start.2
  0.7 0.0 copy-start.1
  0.7 1.5 %first.1 = (f32[8,8,128]{2,1,0:T(8,128)}, f32[48,128]{1,0:T(8,128)S(1)}) custom-call(f32[48,128]{1,0:T(8,128)} %bitcast.22, f32[3,16]{1,0:T(4,128)} %refs_5_.1, f32[1,128]{1,0:T(1,128)} %bitcast.32), custom_call_target="tpu_custom_call" | custom-call | tf_op jit(solution)/shard_map/first/pallas_call | solution.py:546
  2.2 9.0 %all-to-all-start = ((f32[8,8,128]{2,1,0:T(8,128)}), f32[8,8,128]{2,1,0:T(8,128)S(1)}, u32[]{:S(2)}, u32[]{:S(2)}) async-start(f32[8,8,128]{2,1,0:T(8,128)} %get-tuple-element.30), calls=%async_computation | async-start | bytes 65536 | tf_op jit(solution)/shard_map/all_to_all | solution.py:511
  11.9 5.3 %near.4 = (bf16[32,8,128]{2,1,0:T(8,128)(2,1)S(1)}, bf16[6,384,384]{2,1,0:T(8,128)(2,1)S(1)}, s32[32]{0:T(128)S(1)}) custom-call(s32[2,32]{1,0:T(2,128)} %bitcast.36, s32[32]{0:T(128)} %bitcast.40, s32[1]{0:T(128)S(6)} %copy.12.count_ref, f32[48,128]{1,0:T(8,128)S(1)} %get-tuple-element.31.x_ref.refs_1_, bf16[32,384,384]{2,1,0:T(8,128)(2,1)} %b_ref.7), custom_call_target="tpu_custom_call" | custom-call | tf_op jit(solution)/shard_map/near/pallas_call | solution.py:519
  17.1 0.0 copy-start.5
  17.1 1.0 all-to-all-done.rows_ref
  18.1 0.1 join.4
  18.2 17.3 %all_to_all.51 = bf16[32,24,128]{2,1,0:T(8,128)(2,1)S(1)} all-to-all(bf16[32,24,128]{2,1,0:T(8,128)(2,1)S(1)} %join.4), channel_id=1, replica_groups=mesh['row'=8,'col'=32] {'col'}, dimensions={0} | all-to-all | bytes 393216 | tf_op jit(solution)/shard_map/all_to_all | solution.py:543
  35.5 0.0 copy-done.4
  35.5 0.0 copy-done.3
  35.5 0.0 copy-done.2
  35.5 0.0 copy-done.1
  35.5 2.0 %krylov.4 = (bf16[152,512]{1,0:T(8,128)(2,1)S(1)}, f32[4,32,16,128]{3,2,1,0:T(8,128)S(1)}, f32[8,8,128]{2,1,0:T(8,128)}, f32[48,128]{1,0:T(8,128)S(1)}, f32[1,48...) custom-call(bf16[768,128]{1,0:T(8,128)(2,1)S(1)} %bitcast.16, ...), custom_call_target="tpu_custom_call" | custom-call | tf_op jit(solution)/shard_map/krylov/pallas_call | solution.py:580
  37.5 4.8 %all-to-all-start.2 = ((f32[8,8,128]{2,1,0:T(8,128)}), f32[8,8,128]{2,1,0:T(8,128)S(1)}, u32[]{:S(2)}, u32[]{:S(2)}) async-start(f32[8,8,128]{2,1,0:T(8,128)} %get-tuple-element.33), calls=%async_computation.2 | async-start | bytes 65536 | tf_op jit(solution)/shard_map/all_to_all | solution.py:511
  42.3 0.0 copy-done.5
  42.3 4.6 %near.5.near_ref = bf16[32,8,128]{2,1,0:T(8,128)(2,1)S(1)} custom-call(s32[2,32]{1,0:T(2,128)} %bitcast.37, s32[32]{0:T(128)} %copy-done.5, s32[1]{0:T(128)S(6)} %copy.12.count_ref, f32[48,128]{1,0:T(8,128)S(1)} %get-tuple-element.35.x_ref.refs_1_, bf16[32,384,384]{2,1,0:T(8,128)(2,1)} %b_ref.7, bf16[6,384,384]{2,1,0:T(8,128)(2,1)S(1)} %get-tuple-element.36.refs_0_), custom_call_target="tpu_custom_call" | custom-call | tf_op jit(solution)/shard_map/near/pallas_call | solution.py:519
  46.9 2.3 %all-to-all-done.2.rows_ref = f32[8,8,128]{2,1,0:T(8,128)S(1)} async-done(((f32[8,8,128]{2,1,0:T(8,128)}), f32[8,8,128]{2,1,0:T(8,128)S(1)}, u32[]{:S(2)}, u32[]{:S(2)}) %all-to-all-start.2) | async-done | bytes 32800 | tf_op jit(solution)/shard_map/all_to_all | solution.py:511
  49.2 0.1 join.5
  49.3 12.7 %all_to_all.52 = bf16[32,16,128]{2,1,0:T(8,128)(2,1)S(1)} all-to-all(bf16[32,16,128]{2,1,0:T(8,128)(2,1)S(1)} %join.5), channel_id=1, replica_groups=mesh['row'=8,'col'=32] {'col'}, dimensions={0} | all-to-all | bytes 262144 | tf_op jit(solution)/shard_map/all_to_all | solution.py:543
  62.0 1.2 krylov.5
  63.2 3.5 %all-to-all-start.4 = ((f32[8,8,128]{2,1,0:T(8,128)}), f32[8,8,128]{2,1,0:T(8,128)S(1)}, u32[]{:S(2)}, u32[]{:S(2)}) async-start(f32[8,8,128]{2,1,0:T(8,128)} %get-tuple-element.42), calls=%async_computation.4 | async-start | bytes 65536 | tf_op jit(solution)/shard_map/all_to_all | solution.py:511
  66.7 4.6 %near.6.near_ref = bf16[32,8,128]{2,1,0:T(8,128)(2,1)S(1)} custom-call(s32[2,32]{1,0:T(2,128)} %bitcast.38, s32[32]{0:T(128)} %copy-done.5, s32[1]{0:T(128)S(6)} %copy.12.count_ref, f32[48,128]{1,0:T(8,128)S(1)} %get-tuple-element.43.x_ref.refs_1_, bf16[32,384,384]{2,1,0:T(8,128)(2,1)} %b_ref.7, bf16[6,384,384]{2,1,0:T(8,128)(2,1)S(1)} %get-tuple-element.36.refs_0_), custom_call_target="tpu_custom_call" | custom-call | tf_op jit(solution)/shard_map/near/pallas_call | solution.py:519
  71.2 0.0 copy-start
  71.2 2.4 %all-to-all-done.4.rows_ref = f32[8,8,128]{2,1,0:T(8,128)S(1)} async-done(((f32[8,8,128]{2,1,0:T(8,128)}), f32[8,8,128]{2,1,0:T(8,128)S(1)}, u32[]{:S(2)}, u32[]{:S(2)}) %all-to-all-start.4) | async-done | bytes 32800 | tf_op jit(solution)/shard_map/all_to_all | solution.py:511
  73.6 0.1 join.6
  73.7 12.6 %all_to_all.53 = bf16[32,16,128]{2,1,0:T(8,128)(2,1)S(1)} all-to-all(bf16[32,16,128]{2,1,0:T(8,128)(2,1)S(1)} %join.6), channel_id=1, replica_groups=mesh['row'=8,'col'=32] {'col'}, dimensions={0} | all-to-all | bytes 262144 | tf_op jit(solution)/shard_map/all_to_all | solution.py:543
  86.4 1.2 krylov.6
  87.6 3.5 %all-to-all-start.6 = ((f32[8,8,128]{2,1,0:T(8,128)}), f32[8,8,128]{2,1,0:T(8,128)S(1)}, u32[]{:S(2)}, u32[]{:S(2)}) async-start(f32[8,8,128]{2,1,0:T(8,128)} %get-tuple-element.47), calls=%async_computation.6 | async-start | bytes 65536 | tf_op jit(solution)/shard_map/all_to_all | solution.py:511
  91.1 4.6 %near.7.near_ref = bf16[32,8,128]{2,1,0:T(8,128)(2,1)S(1)} custom-call(s32[2,32]{1,0:T(2,128)} %bitcast.39, s32[32]{0:T(128)} %copy-done.5, s32[1]{0:T(128)S(6)} %copy.12.count_ref, f32[48,128]{1,0:T(8,128)S(1)} %get-tuple-element.48.x_ref.refs_1_, bf16[32,384,384]{2,1,0:T(8,128)(2,1)} %b_ref.7, bf16[6,384,384]{2,1,0:T(8,128)(2,1)S(1)} %get-tuple-element.36.refs_0_), custom_call_target="tpu_custom_call" | custom-call | tf_op jit(solution)/shard_map/near/pallas_call | solution.py:519
  95.6 2.4 %all-to-all-done.6.rows_ref = f32[8,8,128]{2,1,0:T(8,128)S(1)} async-done(((f32[8,8,128]{2,1,0:T(8,128)}), f32[8,8,128]{2,1,0:T(8,128)S(1)}, u32[]{:S(2)}, u32[]{:S(2)}) %all-to-all-start.6) | async-done | bytes 32800 | tf_op jit(solution)/shard_map/all_to_all | solution.py:511
  98.0 0.1 join.7
  98.1 12.6 %all_to_all.54 = bf16[32,16,128]{2,1,0:T(8,128)(2,1)S(1)} all-to-all(bf16[32,16,128]{2,1,0:T(8,128)(2,1)S(1)} %join.7), channel_id=1, replica_groups=mesh['row'=8,'col'=32] {'col'}, dimensions={0} | all-to-all | bytes 262144 | tf_op jit(solution)/shard_map/all_to_all | solution.py:543
  110.7 1.1 krylov.7
  111.9 18.9 %all_to_all.55 = f32[256,1,128]{2,1,0:T(1,128)S(1)} all-to-all(f32[256,1,128]{2,1,0:T(1,128)S(1)} %bitcast.21), channel_id=1, replica_groups=mesh['row'=8,'col'=32] {'row','col'}, dimensions={0} | all-to-all | bytes 262144 | tf_op jit(solution)/shard_map/all_to_all | solution.py:593
  130.8 0.0 copy-done
  130.8 0.8 solve.1
Async XLA Ops:
  0.6 34.9 %copy-start.4 = (f32[3,16]{1,0:T(4,128)S(1)}, f32[3,16]{1,0:T(4,128)}, u32[]{:S(2)}) copy-start(f32[3,16]{1,0:T(4,128)} %refs_5_.1) | copy-start | bytes 580
  0.6 34.9 %copy-start.3 = (f32[128]{0:T(128)S(1)}, f32[128]{0:T(128)}, u32[]{:S(2)}) copy-start(f32[128]{0:T(128)} %param.12) | copy-start | bytes 1540
  0.7 34.9 %copy-start.2 = (f32[128]{0:T(128)S(1)}, f32[128]{0:T(128)}, u32[]{:S(2)}) copy-start(f32[128]{0:T(128)} %param.13) | copy-start | bytes 1540
  0.7 34.9 %copy-start.1 = (f32[16]{0:T(128)S(1)}, f32[16]{0:T(128)}, u32[]{:S(2)}) copy-start(f32[16]{0:T(128)} %param.10) | copy-start | bytes 196
  2.2 15.9 %all-to-all-start = ((f32[8,8,128]{2,1,0:T(8,128)}), f32[8,8,128]{2,1,0:T(8,128)S(1)}, u32[]{:S(2)}, u32[]{:S(2)}) async-start(f32[8,8,128]{2,1,0:T(8,128)} %get-tuple-element.30), calls=%async_computation | async-start | bytes 65536 | tf_op jit(solution)/shard_map/all_to_all | solution.py:511
  17.1 25.2 %copy-start.5 = (s32[32]{0:T(128)}, s32[32]{0:T(128)S(1)}, u32[]{:S(2)}) copy-start(s32[32]{0:T(128)S(1)} %get-tuple-element.34.table_hbm) | copy-start | bytes 388
  37.5 11.7 %all-to-all-start.2 = ((f32[8,8,128]{2,1,0:T(8,128)}), f32[8,8,128]{2,1,0:T(8,128)S(1)}, u32[]{:S(2)}, u32[]{:S(2)}) async-start(f32[8,8,128]{2,1,0:T(8,128)} %get-tuple-element.33), calls=%async_computation.2 | async-start | bytes 65536 | tf_op jit(solution)/shard_map/all_to_all | solution.py:511
  63.2 10.4 %all-to-all-start.4 = ((f32[8,8,128]{2,1,0:T(8,128)}), f32[8,8,128]{2,1,0:T(8,128)S(1)}, u32[]{:S(2)}, u32[]{:S(2)}) async-start(f32[8,8,128]{2,1,0:T(8,128)} %get-tuple-element.42), calls=%async_computation.4 | async-start | bytes 65536 | tf_op jit(solution)/shard_map/all_to_all | solution.py:511
  71.2 59.5 %copy-start = (f32[3,16,128]{2,1,0:T(8,128)S(1)}, f32[3,16,128]{2,1,0:T(8,128)}, u32[]{:S(2)}) copy-start(f32[3,16,128]{2,1,0:T(8,128)} %param.9) | copy-start | bytes 73732
  87.6 10.4 %all-to-all-start.6 = ((f32[8,8,128]{2,1,0:T(8,128)}), f32[8,8,128]{2,1,0:T(8,128)S(1)}, u32[]{:S(2)}, u32[]{:S(2)}) async-start(f32[8,8,128]{2,1,0:T(8,128)} %get-tuple-element.47), calls=%async_computation.6 | async-start | bytes 65536 | tf_op jit(solution)/shard_map/all_to_all | solution.py:511
